TPU v7x, 128 devices: a whole 4x4x4 slice. The times are simulated.
128 devices in a mesh: section: 4 (over x), tensor: 32 (over z, y, core).
Axes of the slice: x: 4, y: 4, z: 4, core: 2. Of those that a mesh axis runs over, the one named last changes fastest.
Arguments:
- inputs: bfloat16 [4, 1024, 8192], P('section', None, 'tensor'), may hold values from -6 to 6
- preact: bfloat16 [4, 1024, 32768], P('section', None, 'tensor'), may hold values from -6 to 6
- handoff: bfloat16 [4, 1024, 8192], P('section', None, 'tensor'), may hold values from -6 to 6
- first_blocks: bfloat16 [4, 128, 6, 256, 256], P('section', 'tensor'), may hold values from -0.15625 to 0.15625
- second_blocks: bfloat16 [4, 128, 6, 256, 256], P('section', 'tensor'), may hold values from -0.078125 to 0.078125
- left_one: bfloat16 [4, 8192, 256], P('section', 'tensor'), may hold values from -0.0625 to 0.0625
- right_one: bfloat16 [4, 256, 32768], P('section', None, 'tensor'), may hold values from -0.375 to 0.375
- left_two: bfloat16 [4, 32768, 256], P('section', 'tensor'), may hold values from -0.03125 to 0.03125
- right_two: bfloat16 [4, 256, 8192], P('section', None, 'tensor'), may hold values from -0.375 to 0.375
Outputs:
- input_grad: bfloat16 [4, 1024, 8192], P('section', None, 'tensor')
- first_grad: bfloat16 [4, 128, 6, 256, 256], P('section', 'tensor')
- second_grad: bfloat16 [4, 128, 6, 256, 256], P('section', 'tensor')
- leftone_grad: bfloat16 [4, 8192, 256], P('section', 'tensor')
- rightone_grad: bfloat16 [4, 256, 32768], P('section', None, 'tensor')
- lefttwo_grad: bfloat16 [4, 32768, 256], P('section', 'tensor')
- righttwo_grad: bfloat16 [4, 256, 8192], P('section', None, 'tensor')
All inputs are finite; a program needn't handle non-finite values.
Results may differ from a plain program's by a relative error of at most 0.0061.
Values may be sent and summed in bfloat16 or wider, within the bound.
A program may use at most 128 MiB of HBM per device.

v0:
```python
import jax
import jax.numpy as jnp
from jax import lax
from jax.sharding import PartitionSpec as P


def swapped(value, axis, apart):
    mask = 2**apart
    pairs = [(source, source ^ mask) for source in range(lax.axis_size(axis))]
    return lax.ppermute(value, axis, pairs)


def shifted(shard, axis, by):
    peers = lax.axis_size(axis)
    return lax.ppermute(shard, axis, [(i, (i + by) % peers) for i in range(peers)])


def gelu_pair(preact):
    values = preact.astype(jnp.float32)
    normal_cdf = 0.5 * (1.0 + jax.scipy.special.erf(values * 0.7071067811865476))
    density = jnp.exp(-0.5 * values * values) * 0.3989422804014327
    return (values * normal_cdf, normal_cdf + values * density)


def partner_sets(values, count_in, link_count, swapper):
    local_bits = count_in.bit_length() - 1
    result = [values]
    for degree in range(1, link_count):
        result.append(swapper(values, degree - 1 - local_bits))
    return result


def body(
    inputs, preact, handoff, first_blocks, second_blocks, left_one, right_one, left_two, right_two
):
    own_inputs = inputs[0]
    blocks_one = first_blocks[0]
    blocks_two = second_blocks[0]
    hid_count = blocks_one.shape[0]
    link_count = blocks_one.shape[1]
    block_size = blocks_one.shape[-1]
    row_count = own_inputs.shape[0]
    feat_width = own_inputs.shape[1]
    count_in = feat_width // block_size
    group_size = hid_count // count_in
    local_bits = count_in.bit_length() - 1
    activated, slope_vals = gelu_pair(preact[0])
    activated = activated.astype(jnp.bfloat16)
    proj_in, proj_act = lax.psum(
        (
            jnp.dot(own_inputs, left_one[0], preferred_element_type=jnp.float32),
            jnp.dot(activated, left_two[0], preferred_element_type=jnp.float32),
        ),
        "tensor",
    )
    proj_in = proj_in.astype(jnp.bfloat16)
    proj_act = proj_act.astype(jnp.bfloat16)

    def swap_inputs(values, bit_pos):
        return swapped(values, "tensor", bit_pos)

    def swap_grads(values, bit_pos):
        return swapped(values, "tensor", bit_pos)

    input_sets = jnp.stack(partner_sets(own_inputs, count_in, link_count, swap_inputs))
    upstream = shifted(handoff[0], "section", -1)
    grad_sets = jnp.stack(partner_sets(upstream, count_in, link_count, swap_grads))
    proj_grad = lax.psum(
        jnp.dot(upstream, right_two[0].T, preferred_element_type=jnp.float32), "tensor"
    ).astype(jnp.bfloat16)
    grad_view = grad_sets.reshape(link_count, row_count, count_in, block_size)
    second_view = blocks_two.reshape(count_in, group_size, link_count, block_size, block_size)
    grad_act = jnp.einsum(
        "ktcb,cjkeb->tcje", grad_view, second_view, preferred_element_type=jnp.float32
    ).reshape(row_count, hid_count * block_size)
    grad_act = grad_act + jnp.dot(proj_grad, left_two[0].T, preferred_element_type=jnp.float32)
    hidden_grad = (grad_act * slope_vals).astype(jnp.bfloat16)
    back_rank = lax.psum(
        jnp.dot(hidden_grad, right_one[0].T, preferred_element_type=jnp.float32), "tensor"
    ).astype(jnp.bfloat16)
    hidden_view = hidden_grad.reshape(row_count, count_in, group_size, block_size)
    first_view = blocks_one.reshape(count_in, group_size, link_count, block_size, block_size)
    partials = jnp.einsum(
        "tcje,cjkbe->ktcb", hidden_view, first_view, preferred_element_type=jnp.float32
    ).reshape(link_count, row_count, feat_width)
    summed_grad = partials[0] + jnp.dot(
        back_rank, left_one[0].T, preferred_element_type=jnp.float32
    )
    degree_order = list(range(1, link_count))
    for degree in degree_order:
        summed_grad = summed_grad + swapped(partials[degree], "tensor", degree - 1 - local_bits)
    input_grad = summed_grad.astype(jnp.bfloat16)[None]
    input_view = input_sets.reshape(link_count, row_count, count_in, block_size)
    first_grad = jnp.einsum(
        "ktcb,tcje->cjkbe", input_view, hidden_view, preferred_element_type=jnp.float32
    )
    first_grad = first_grad.reshape(hid_count, link_count, block_size, block_size).astype(
        jnp.bfloat16
    )[None]
    activ_view = activated.reshape(row_count, count_in, group_size, block_size)
    second_grad = jnp.einsum(
        "tcje,ktcb->cjkeb", activ_view, grad_view, preferred_element_type=jnp.float32
    )
    second_grad = second_grad.reshape(hid_count, link_count, block_size, block_size).astype(
        jnp.bfloat16
    )[None]
    leftone_grad = jnp.dot(own_inputs.T, back_rank, preferred_element_type=jnp.float32).astype(
        jnp.bfloat16
    )[None]
    rightone_grad = jnp.dot(proj_in.T, hidden_grad, preferred_element_type=jnp.float32).astype(
        jnp.bfloat16
    )[None]
    lefttwo_grad = jnp.dot(activated.T, proj_grad, preferred_element_type=jnp.float32).astype(
        jnp.bfloat16
    )[None]
    righttwo_grad = jnp.dot(proj_act.T, upstream, preferred_element_type=jnp.float32).astype(
        jnp.bfloat16
    )[None]
    return (
        input_grad,
        first_grad,
        second_grad,
        leftone_grad,
        rightone_grad,
        lefttwo_grad,
        righttwo_grad,
    )


def solution(mesh):
    in_specs = (
        P("section", None, "tensor"),
        P("section", None, "tensor"),
        P("section", None, "tensor"),
        P("section", "tensor", None, None, None),
        P("section", "tensor", None, None, None),
        P("section", "tensor", None),
        P("section", None, "tensor"),
        P("section", "tensor", None),
        P("section", None, "tensor"),
    )
    out_specs = (
        P("section", None, "tensor"),
        P("section", "tensor", None, None, None),
        P("section", "tensor", None, None, None),
        P("section", "tensor", None),
        P("section", None, "tensor"),
        P("section", "tensor", None),
        P("section", None, "tensor"),
    )
    return jax.shard_map(body, mesh=mesh, in_specs=in_specs, out_specs=out_specs, check_vma=False)
```

profile of v0, /device:TPU:1, one launch (start us, length us, event | category | flops | bytes accessed | tf_op | source)
XLA Modules:
  0.0 437.1 jit_solution(17502697164771448957)
XLA Ops:
  0.6 0.0 copy-start
  0.7 4.5 %collective-permute-start.15 = (bf16[1024,256]{1,0:T(8,128)(2,1)}, bf16[1024,256]{1,0:T(8,128)(2,1)}, u32[]{:S(2)}, u32[]{:S(2)}) collective-permute-start(bf16[1024,256]{1,0:T(8,128)(2,1)} %bitcast.45), channel_id=1, source_target_pairs={{0,16},{1,17},{2,18},{3,19},{4,20},{5,21},{6,22},{7,23},{8,24},{9,... | collective-permute-start | bytes 1572872 | tf_op jit(solution)/shard_map/ppermute | solution.py:10
  5.1 0.7 collective-permute-start.14
  5.9 2.9 collective-permute-start.13
  8.8 0.4 collective-permute-start.12
  9.2 2.5 collective-permute-start
  11.7 3.9 copy.16
  15.6 2.3 fusion.17
  18.0 2.7 fusion.64
  20.7 1.8 fusion.33
  22.4 1.9 constant_dynamic-update-slice_fusion
  24.3 0.0 collective-permute-done
  24.3 2.1 collective-permute-start.11
  26.4 2.3 fusion.67
  28.7 129.8 %all-reduce.3 = bf16[1024,256]{1,0:T(8,128)(2,1)} all-reduce(f32[1024,256]{1,0:T(8,128)} %fusion.67), channel_id=1, replica_groups=mesh['section'=4,'tensor'=32] {'tensor'}, use_global_device_ids=true, to_apply=%region_0.0 | all-reduce | flops 262144 | bytes 1572864 | tf_op jit(solution)/shard_map/psum | solution.py:68
  158.5 3.7 fusion.45
  162.3 1.1 bitcast_dynamic-update-slice_fusion.10
  163.4 0.0 collective-permute-done.11
  163.4 0.1 collective-permute-start.5
  163.5 1.1 bitcast_dynamic-update-slice_fusion.4
  164.6 0.0 collective-permute-done.12
  164.6 0.1 collective-permute-start.4
  164.7 1.1 bitcast_dynamic-update-slice_fusion.3
  165.7 0.0 collective-permute-done.13
  165.7 5.9 %collective-permute-start.1 = (bf16[1024,256]{1,0:T(8,128)(2,1)}, bf16[1024,256]{1,0:T(8,128)(2,1)S(1)}, u32[]{:S(2)}, u32[]{:S(2)}) collective-permute-start(bf16[1024,256]{1,0:T(8,128)(2,1)} %collective-permute-done), channel_id=1, source_target_pairs={{0,1},{1,0},{2,3},{3,2},{4,5},{5,4},{6,7},{7,6},{8,9},{9,8},{10,11... | collective-permute-start | bytes 1572872 | tf_op jit(solution)/shard_map/ppermute | solution.py:10
  171.6 1.1 bitcast_dynamic-update-slice_fusion.2
  172.7 0.0 collective-permute-done.14
  172.7 0.1 collective-permute-start.2
  172.8 1.1 bitcast_dynamic-update-slice_fusion.1
  173.9 2.2 collective-permute-start.3
  176.1 1.1 bitcast_dynamic-update-slice_fusion
  177.2 0.0 collective-permute-done.1
  177.2 9.2 %collective-permute-done.2 = bf16[1024,256]{1,0:T(8,128)(2,1)S(1)} collective-permute-done((bf16[1024,256]{1,0:T(8,128)(2,1)}, bf16[1024,256]{1,0:T(8,128)(2,1)S(1)}, u32[]{:S(2)}, u32[]{:S(2)}) %collective-permute-start.2) | collective-permute-done | bytes 524320 | tf_op jit(solution)/shard_map/ppermute | solution.py:10
  186.5 11.5 %collective-permute-done.3 = bf16[1024,256]{1,0:T(8,128)(2,1)S(1)} collective-permute-done((bf16[1024,256]{1,0:T(8,128)(2,1)}, bf16[1024,256]{1,0:T(8,128)(2,1)S(1)}, u32[]{:S(2)}, u32[]{:S(2)}) %collective-permute-start.3) | collective-permute-done | bytes 524320 | tf_op jit(solution)/shard_map/ppermute | solution.py:10
  198.1 0.0 collective-permute-done.5
  198.2 0.0 copy-start.13
  198.2 1.7 copy-done.13
  199.8 4.9 %convert_bitcast_fusion.1 = bf16[1,4,6,256,256]{3,4,1,2,0:T(8,128)(2,1)} fusion(bf16[1024,4,256,1]{0,2,1,3:T(8,128)(2,1)S(1)} %bitcast.207, bf16[6,1024,256]{2,1,0:T(8,128)(2,1)S(1)} %bitcast_dynamic-update-slice_fusion.5), kind=kOutput, calls=%fused_computation.31 | convolution fusion | flops 3222798336 | bytes 8388608 | tf_op jit(solution)/shard_map/tcje,ktcb->cjkeb/dot_general | solution.py:101
  204.7 4.6 %copy.27 = bf16[1,4,6,256,256]{4,3,2,1,0:T(8,128)(2,1)} copy(bf16[1,4,6,256,256]{3,4,1,2,0:T(8,128)(2,1)} %convert_bitcast_fusion.1) | data formatting | bytes 6291456
  209.4 6.4 %fusion.24 = f32[1024,4,256,1]{0,2,3,1:T(8,128)S(1)} fusion(bf16[1,4,6,256,256]{4,3,2,1,0:T(8,128)(2,1)} %param.13, bf16[6,1024,256]{2,1,0:T(8,128)(2,1)} %copy-done.13), kind=kOutput, calls=%fused_computation.28 | convolution fusion | flops 3221225472 | bytes 10485760 | tf_op jit(solution)/shard_map/ktcb,cjkeb->tcje/dot_general | solution.py:73
  215.8 0.0 copy-start.10
  215.8 2.4 fusion.12
  218.3 1.3 copy-done.4
  219.6 1.7 fusion.51
  221.4 147.7 %all-reduce.4 = (bf16[1024,256]{1,0:T(8,128)(2,1)}, bf16[1024,256]{1,0:T(8,128)(2,1)}, bf16[1024,256]{1,0:T(8,128)(2,1)}) all-reduce(f32[1024,256]{1,0:T(8,128)} %fusion.51, f32[1024,256]{1,0:T(8,128)} %fusion.64, f32[1024,256]{1,0:T(8,128)} %fusion.33), channel_id=1, replica_groups=mesh['section'=4,'tensor'=32] {'tensor'}, use_global_device_ids=true, to_apply=%region_1.0 | all-reduce | flops 786432 | bytes 4718592 | tf_op jit(solution)/shard_map/psum | solution.py:78
  369.1 1.5 fusion.49
  370.6 0.8 copy.28
  371.4 5.1 %fusion.22 = f32[1024,6,256,1]{2,0,1,3:T(8,128)S(1)} fusion(bf16[1024,4,256,1]{0,2,3,1:T(8,128)(2,1)} %bitcast.205, bf16[1,4,6,256,256]{4,3,2,1,0:T(8,128)(2,1)S(1)} %copy-done), kind=kOutput, calls=%fused_computation.26 | convolution fusion | flops 3221225472 | bytes 11534336 | tf_op jit(solution)/shard_map/tcje,cjkbe->ktcb/dot_general | solution.py:83
  376.5 1.2 slice_bitcast_fusion
  377.7 2.1 slice_bitcast_fusion.4
  379.7 1.8 copy-done.3
  381.5 5.8 %collective-permute-start.6 = (f32[1024,256]{1,0:T(8,128)}, f32[1024,256]{1,0:T(8,128)}, u32[]{:S(2)}, u32[]{:S(2)}) collective-permute-start(f32[1024,256]{1,0:T(8,128)} %get-tuple-element.17), channel_id=1, source_target_pairs={{0,1},{1,0},{2,3},{3,2},{4,5},{5,4},{6,7},{7,6},{8,9},{9,8},{10,11... | collective-permute-start | bytes 3145736 | tf_op jit(solution)/shard_map/ppermute | solution.py:10
  387.4 0.0 collective-permute-start.9
  387.4 0.0 collective-permute-start.8
  387.4 0.0 collective-permute-start.7
  387.4 4.9 %convert_bitcast_fusion.2 = bf16[1,4,6,256,256]{3,4,2,1,0:T(8,128)(2,1)} fusion(bf16[1024,4,256,1]{0,2,3,1:T(8,128)(2,1)S(1)} %bitcast.206, bf16[6,1024,256]{2,1,0:T(8,128)(2,1)S(1)} %copy-done.16), kind=kOutput, calls=%fused_computation.32 | convolution fusion | flops 3222798336 | bytes 8388608 | tf_op jit(solution)/shard_map/ktcb,tcje->cjkbe/dot_general | solution.py:94
  392.3 4.7 %copy.26 = bf16[1,4,6,256,256]{4,3,2,1,0:T(8,128)(2,1)} copy(bf16[1,4,6,256,256]{3,4,2,1,0:T(8,128)(2,1)} %convert_bitcast_fusion.2) | data formatting | bytes 6291456
  397.0 2.1 fusion.50
  399.1 3.5 fusion.44
  402.6 0.0 collective-permute-done.10
  402.6 0.0 collective-permute-done.6
  402.6 14.8 %collective-permute-done.9 = f32[1024,256]{1,0:T(8,128)} collective-permute-done((f32[1024,256]{1,0:T(8,128)}, f32[1024,256]{1,0:T(8,128)}, u32[]{:S(2)}, u32[]{:S(2)}) %collective-permute-start.9) | collective-permute-done | bytes 1048608 | tf_op jit(solution)/shard_map/ppermute | solution.py:10
  417.4 15.6 %collective-permute-done.7 = f32[1024,256]{1,0:T(8,128)} collective-permute-done((f32[1024,256]{1,0:T(8,128)}, f32[1024,256]{1,0:T(8,128)}, u32[]{:S(2)}, u32[]{:S(2)}) %collective-permute-start.7) | collective-permute-done | bytes 1048608 | tf_op jit(solution)/shard_map/ppermute | solution.py:10
  433.0 4.1 fusion.48
  (43 shorter events, 0.3 us)
Async XLA Ops:
  0.6 370.8 %copy-start = (bf16[1,4,6,256,256]{4,3,2,1,0:T(8,128)(2,1)S(1)}, bf16[1,4,6,256,256]{4,3,2,1,0:T(8,128)(2,1)}, u32[]{:S(2)}) copy-start(bf16[1,4,6,256,256]{4,3,2,1,0:T(8,128)(2,1)} %param.12) | copy-start | bytes 9437188
  0.7 173.3 %collective-permute-start.15 = (bf16[1024,256]{1,0:T(8,128)(2,1)}, bf16[1024,256]{1,0:T(8,128)(2,1)}, u32[]{:S(2)}, u32[]{:S(2)}) collective-permute-start(bf16[1024,256]{1,0:T(8,128)(2,1)} %bitcast.45), channel_id=1, source_target_pairs={{0,16},{1,17},{2,18},{3,19},{4,20},{5,21},{6,22},{7,23},{8,24},{9,... | collective-permute-start | bytes 1572872 | tf_op jit(solution)/shard_map/ppermute | solution.py:10
  5.1 167.6 %collective-permute-start.14 = (bf16[1024,256]{1,0:T(8,128)(2,1)}, bf16[1024,256]{1,0:T(8,128)(2,1)}, u32[]{:S(2)}, u32[]{:S(2)}) collective-permute-start(bf16[1024,256]{1,0:T(8,128)(2,1)} %bitcast.45), channel_id=1, source_target_pairs={{0,8},{1,9},{2,10},{3,11},{4,12},{5,13},{6,14},{7,15},{8,0},{9,1},... | collective-permute-start | bytes 1572872 | tf_op jit(solution)/shard_map/ppermute | solution.py:10
  5.9 159.9 %collective-permute-start.13 = (bf16[1024,256]{1,0:T(8,128)(2,1)}, bf16[1024,256]{1,0:T(8,128)(2,1)}, u32[]{:S(2)}, u32[]{:S(2)}) collective-permute-start(bf16[1024,256]{1,0:T(8,128)(2,1)} %bitcast.45), channel_id=1, source_target_pairs={{0,4},{1,5},{2,6},{3,7},{4,0},{5,1},{6,2},{7,3},{8,12},{9,13},{10,... | collective-permute-start | bytes 1572872 | tf_op jit(solution)/shard_map/ppermute | solution.py:10
  8.8 155.8 %collective-permute-start.12 = (bf16[1024,256]{1,0:T(8,128)(2,1)}, bf16[1024,256]{1,0:T(8,128)(2,1)}, u32[]{:S(2)}, u32[]{:S(2)}) collective-permute-start(bf16[1024,256]{1,0:T(8,128)(2,1)} %bitcast.45), channel_id=1, source_target_pairs={{0,2},{1,3},{2,0},{3,1},{4,6},{5,7},{6,4},{7,5},{8,10},{9,11},{10,... | collective-permute-start | bytes 1572872 | tf_op jit(solution)/shard_map/ppermute | solution.py:10
  9.2 8.7 %copy-start.9 = (bf16[1,256,256]{2,1,0:T(8,128)(2,1)S(1)}, bf16[1,256,256]{2,1,0:T(8,128)(2,1)}, u32[]{:S(2)}) copy-start(bf16[1,256,256]{2,1,0:T(8,128)(2,1)} %param.14) | copy-start | bytes 393220
  9.2 15.1 %collective-permute-start = (bf16[1024,256]{1,0:T(8,128)(2,1)}, bf16[1024,256]{1,0:T(8,128)(2,1)}, u32[]{:S(2)}, u32[]{:S(2)}) collective-permute-start(bf16[1024,256]{1,0:T(8,128)(2,1)} %bitcast.208), channel_id=1, source_target_pairs={{0,96},{32,0},{64,32},{96,64},{1,97},{33,1},{65,33},{97,65},{2,98}... | collective-permute-start | bytes 1572872 | tf_op jit(solution)/shard_map/ppermute | solution.py:15
  15.6 5.0 %copy-start.17 = (bf16[1,1024,256]{2,1,0:T(8,128)(2,1)S(1)}, bf16[1,1024,256]{2,1,0:T(8,128)(2,1)}, u32[]{:S(2)}) copy-start(bf16[1,1024,256]{2,1,0:T(8,128)(2,1)} %param.16) | copy-start | bytes 1572868
  17.9 4.5 %copy-start.6 = (bf16[1,1024,1024]{1,2,0:T(8,128)(2,1)}, bf16[1,1024,1024]{1,2,0:T(8,128)(2,1)S(1)}, u32[]{:S(2)}) copy-start(bf16[1,1024,1024]{1,2,0:T(8,128)(2,1)S(1)} %fusion.17) | copy-start | bytes 6291460
  20.7 5.7 %copy-start.12 = (bf16[1,256,256]{2,1,0:T(8,128)(2,1)S(1)}, bf16[1,256,256]{2,1,0:T(8,128)(2,1)}, u32[]{:S(2)}) copy-start(bf16[1,256,256]{2,1,0:T(8,128)(2,1)} %param.17) | copy-start | bytes 393220
  24.3 139.1 %collective-permute-start.11 = (bf16[1024,256]{1,0:T(8,128)(2,1)}, bf16[1024,256]{1,0:T(8,128)(2,1)}, u32[]{:S(2)}, u32[]{:S(2)}) collective-permute-start(bf16[1024,256]{1,0:T(8,128)(2,1)} %bitcast.45), channel_id=1, source_target_pairs={{0,1},{1,0},{2,3},{3,2},{4,5},{5,4},{6,7},{7,6},{8,9},{9,8},{10,11... | collective-permute-start | bytes 1572872 | tf_op jit(solution)/shard_map/ppermute | solution.py:10
  158.5 4.9 %copy-start.14 = (bf16[6,1024,256]{2,1,0:T(8,128)(2,1)S(1)}, bf16[6,1024,256]{2,1,0:T(8,128)(2,1)}, u32[]{:S(2)}) copy-start(bf16[6,1024,256]{2,1,0:T(8,128)(2,1)} %constant_dynamic-update-slice_fusion) | copy-start | bytes 9437188
  163.4 34.7 %collective-permute-start.5 = (bf16[1024,256]{1,0:T(8,128)(2,1)}, bf16[1024,256]{1,0:T(8,128)(2,1)S(1)}, u32[]{:S(2)}, u32[]{:S(2)}) collective-permute-start(bf16[1024,256]{1,0:T(8,128)(2,1)} %collective-permute-done), channel_id=1, source_target_pairs={{0,16},{1,17},{2,18},{3,19},{4,20},{5,21},{6,22},{7,23},{8,24},{9,... | collective-permute-start | bytes 1572872 | tf_op jit(solution)/shard_map/ppermute | solution.py:10
  164.6 33.5 %collective-permute-start.4 = (bf16[1024,256]{1,0:T(8,128)(2,1)}, bf16[1024,256]{1,0:T(8,128)(2,1)S(1)}, u32[]{:S(2)}, u32[]{:S(2)}) collective-permute-start(bf16[1024,256]{1,0:T(8,128)(2,1)} %collective-permute-done), channel_id=1, source_target_pairs={{0,8},{1,9},{2,10},{3,11},{4,12},{5,13},{6,14},{7,15},{8,0},{9,1},... | collective-permute-start | bytes 1572872 | tf_op jit(solution)/shard_map/ppermute | solution.py:10
  165.7 11.4 %collective-permute-start.1 = (bf16[1024,256]{1,0:T(8,128)(2,1)}, bf16[1024,256]{1,0:T(8,128)(2,1)S(1)}, u32[]{:S(2)}, u32[]{:S(2)}) collective-permute-start(bf16[1024,256]{1,0:T(8,128)(2,1)} %collective-permute-done), channel_id=1, source_target_pairs={{0,1},{1,0},{2,3},{3,2},{4,5},{5,4},{6,7},{7,6},{8,9},{9,8},{10,11... | collective-permute-start | bytes 1572872 | tf_op jit(solution)/shard_map/ppermute | solution.py:10
  172.7 13.8 %collective-permute-start.2 = (bf16[1024,256]{1,0:T(8,128)(2,1)}, bf16[1024,256]{1,0:T(8,128)(2,1)S(1)}, u32[]{:S(2)}, u32[]{:S(2)}) collective-permute-start(bf16[1024,256]{1,0:T(8,128)(2,1)} %collective-permute-done), channel_id=1, source_target_pairs={{0,2},{1,3},{2,0},{3,1},{4,6},{5,7},{6,4},{7,5},{8,10},{9,11},{10,... | collective-permute-start | bytes 1572872 | tf_op jit(solution)/shard_map/ppermute | solution.py:10
  173.9 25.9 %copy-start.7 = (bf16[1,1024,1024]{1,2,0:T(8,128)(2,1)S(1)}, bf16[1,1024,1024]{1,2,0:T(8,128)(2,1)}, u32[]{:S(2)}) copy-start(bf16[1,1024,1024]{1,2,0:T(8,128)(2,1)} %copy-done.6) | copy-start | bytes 6291460
  173.9 24.1 %collective-permute-start.3 = (bf16[1024,256]{1,0:T(8,128)(2,1)}, bf16[1024,256]{1,0:T(8,128)(2,1)S(1)}, u32[]{:S(2)}, u32[]{:S(2)}) collective-permute-start(bf16[1024,256]{1,0:T(8,128)(2,1)} %collective-permute-done), channel_id=1, source_target_pairs={{0,4},{1,5},{2,6},{3,7},{4,0},{5,1},{6,2},{7,3},{8,12},{9,13},{10,... | collective-permute-start | bytes 1572872 | tf_op jit(solution)/shard_map/ppermute | solution.py:10
  177.2 21.0 %copy-start.15 = (bf16[6,1024,256]{2,1,0:T(8,128)(2,1)}, bf16[6,1024,256]{2,1,0:T(8,128)(2,1)S(1)}, u32[]{:S(2)}) copy-start(bf16[6,1024,256]{2,1,0:T(8,128)(2,1)S(1)} %bitcast_dynamic-update-slice_fusion) | copy-start | bytes 9437188
  198.2 1.7 copy-start.13
  209.4 6.4 %copy-start.2 = (bf16[1,1024,1024]{1,2,0:T(8,128)(2,1)S(1)}, bf16[1,1024,1024]{1,2,0:T(8,128)(2,1)}, u32[]{:S(2)}) copy-start(bf16[1,1024,1024]{1,2,0:T(8,128)(2,1)} %copy.16) | copy-start | bytes 6291460
  209.4 6.4 %copy-start.11 = (bf16[1024,256]{1,0:T(8,128)(2,1)S(1)}, bf16[1024,256]{1,0:T(8,128)(2,1)}, u32[]{:S(2)}) copy-start(bf16[1024,256]{1,0:T(8,128)(2,1)} %all-reduce.3) | copy-start | bytes 1572868
  209.4 6.4 %copy-start.18 = (bf16[1,1024,256]{2,1,0:T(8,128)(2,1)S(1)}, bf16[1,1024,256]{2,1,0:T(8,128)(2,1)}, u32[]{:S(2)}) copy-start(bf16[1,1024,256]{2,1,0:T(8,128)(2,1)} %param.16) | copy-start | bytes 1572868
  215.8 3.8 copy-start.10
  218.3 1.3 copy-start.4
  376.5 5.1 %copy-start.3 = (f32[1024,6,256,1]{2,0,1,3:T(8,128)}, f32[1024,6,256,1]{2,0,1,3:T(8,128)S(1)}, u32[]{:S(2)}) copy-start(f32[1024,6,256,1]{2,0,1,3:T(8,128)S(1)} %fusion.22) | copy-start | bytes 18874372
  377.6 24.9 %collective-permute-start.10 = (f32[1024,256]{1,0:T(8,128)}, f32[1024,256]{1,0:T(8,128)}, u32[]{:S(2)}, u32[]{:S(2)}) collective-permute-start(f32[1024,256]{1,0:T(8,128)} %slice_bitcast_fusion), channel_id=1, source_target_pairs={{0,16},{1,17},{2,18},{3,19},{4,20},{5,21},{6,22},{7,23},{8,24},{9,... | collective-permute-start | bytes 3145736 | tf_op jit(solution)/shard_map/ppermute | solution.py:10
  377.6 9.7 %copy-start.5 = (bf16[1024,1024]{0,1:T(8,128)(2,1)S(1)}, bf16[1024,1024]{0,1:T(8,128)(2,1)}, u32[]{:S(2)}) copy-start(bf16[1024,1024]{0,1:T(8,128)(2,1)} %copy-done.4) | copy-start | bytes 6291460
  377.7 9.8 %copy-start.16 = (bf16[6,1024,256]{2,1,0:T(8,128)(2,1)S(1)}, bf16[6,1024,256]{2,1,0:T(8,128)(2,1)}, u32[]{:S(2)}) copy-start(bf16[6,1024,256]{2,1,0:T(8,128)(2,1)} %copy-done.15) | copy-start | bytes 9437188
  381.5 21.0 %collective-permute-start.6 = (f32[1024,256]{1,0:T(8,128)}, f32[1024,256]{1,0:T(8,128)}, u32[]{:S(2)}, u32[]{:S(2)}) collective-permute-start(f32[1024,256]{1,0:T(8,128)} %get-tuple-element.17), channel_id=1, source_target_pairs={{0,1},{1,0},{2,3},{3,2},{4,5},{5,4},{6,7},{7,6},{8,9},{9,8},{10,11... | collective-permute-start | bytes 3145736 | tf_op jit(solution)/shard_map/ppermute | solution.py:10
  387.4 30.0 %collective-permute-start.9 = (f32[1024,256]{1,0:T(8,128)}, f32[1024,256]{1,0:T(8,128)}, u32[]{:S(2)}, u32[]{:S(2)}) collective-permute-start(f32[1024,256]{1,0:T(8,128)} %get-tuple-element.18), channel_id=1, source_target_pairs={{0,8},{1,9},{2,10},{3,11},{4,12},{5,13},{6,14},{7,15},{8,0},{9,1},... | collective-permute-start | bytes 3145736 | tf_op jit(solution)/shard_map/ppermute | solution.py:10
  387.4 30.0 %collective-permute-start.8 = (f32[1024,256]{1,0:T(8,128)}, f32[1024,256]{1,0:T(8,128)}, u32[]{:S(2)}, u32[]{:S(2)}) collective-permute-start(f32[1024,256]{1,0:T(8,128)} %get-tuple-element.19), channel_id=1, source_target_pairs={{0,4},{1,5},{2,6},{3,7},{4,0},{5,1},{6,2},{7,3},{8,12},{9,13},{10,... | collective-permute-start | bytes 3145736 | tf_op jit(solution)/shard_map/ppermute | solution.py:10
  387.4 45.6 %collective-permute-start.7 = (f32[1024,256]{1,0:T(8,128)}, f32[1024,256]{1,0:T(8,128)}, u32[]{:S(2)}, u32[]{:S(2)}) collective-permute-start(f32[1024,256]{1,0:T(8,128)} %get-tuple-element.20), channel_id=1, source_target_pairs={{0,2},{1,3},{2,0},{3,1},{4,6},{5,7},{6,4},{7,5},{8,10},{9,11},{10,... | collective-permute-start | bytes 3145736 | tf_op jit(solution)/shard_map/ppermute | solution.py:10
  392.3 4.7 %copy-start.19 = (bf16[1024,256]{1,0:T(8,128)(2,1)S(1)}, bf16[1024,256]{1,0:T(8,128)(2,1)}, u32[]{:S(2)}) copy-start(bf16[1024,256]{1,0:T(8,128)(2,1)} %get-tuple-element.16) | copy-start | bytes 1572868
  397.0 36.0 %copy-start.8 = (bf16[1024,256]{1,0:T(8,128)(2,1)S(1)}, bf16[1024,256]{1,0:T(8,128)(2,1)}, u32[]{:S(2)}) copy-start(bf16[1024,256]{1,0:T(8,128)(2,1)} %get-tuple-element.14) | copy-start | bytes 1572868
  399.1 38.0 %copy-start.1 = (bf16[1,4,6,256,256]{4,3,2,1,0:T(8,128)(2,1)S(1)}, bf16[1,4,6,256,256]{4,3,2,1,0:T(8,128)(2,1)}, u32[]{:S(2)}) copy-start(bf16[1,4,6,256,256]{4,3,2,1,0:T(8,128)(2,1)} %param.12) | copy-start | bytes 9437188
where the time goes:
time: 438 us; the launch traced here: 437 us
  blocking collectives  278 us (63%)
  waiting for transfers between devices  51.1 us (12%)
  matrix products  47.2 us (11%)
  local copies, waits for them, and re-layouts  30.6 us (7%)
  starting transfers between devices  27.3 us (6%)
    psum x1, blocking collectives, body(): lax.psum(jnp.dot(hidden_grad, right_one[0].T, preferred_element_type=jnp....  148 us
    psum x1, blocking collectives, body(): lax.psum(jnp.dot(upstream, right_two[0].T, preferred_element_type=jnp.flo...  130 us
    ppermute x15, waiting for transfers between devices, swapped(): return lax.ppermute(value, axis, pairs)  51.1 us
    unnamed x54, local copies, waits for them, and re-layouts  26.3 us
    ppermute x15, starting transfers between devices, swapped(): return lax.ppermute(value, axis, pairs)  24.8 us
  transfers between devices with their start and end apart: 16, of which 4 were waited for; matrix products, arithmetic and copies ran while one was open for 10% of the time, Pallas kernels for 0%

commit v1 on v0

--- a/solution.py
+++ b/solution.py
@@ -13,6 +13,11 @@
 def shifted(shard, axis, by):
     peers = lax.axis_size(axis)
     return lax.ppermute(shard, axis, [(i, (i + by) % peers) for i in range(peers)])
+
+
+def summed(values):
+    part = lax.psum_scatter(values, "tensor", scatter_dimension=0, tiled=True)
+    return lax.all_gather(part.astype(jnp.bfloat16), "tensor", axis=0, tiled=True)
 
 
 def gelu_pair(preact):
@@ -46,15 +51,8 @@
     local_bits = count_in.bit_length() - 1
     activated, slope_vals = gelu_pair(preact[0])
     activated = activated.astype(jnp.bfloat16)
-    proj_in, proj_act = lax.psum(
-        (
-            jnp.dot(own_inputs, left_one[0], preferred_element_type=jnp.float32),
-            jnp.dot(activated, left_two[0], preferred_element_type=jnp.float32),
-        ),
-        "tensor",
-    )
-    proj_in = proj_in.astype(jnp.bfloat16)
-    proj_act = proj_act.astype(jnp.bfloat16)
+    proj_in = summed(jnp.dot(own_inputs, left_one[0], preferred_element_type=jnp.float32))
+    proj_act = summed(jnp.dot(activated, left_two[0], preferred_element_type=jnp.float32))
 
     def swap_inputs(values, bit_pos):
         return swapped(values, "tensor", bit_pos)
@@ -65,9 +63,7 @@
     input_sets = jnp.stack(partner_sets(own_inputs, count_in, link_count, swap_inputs))
     upstream = shifted(handoff[0], "section", -1)
     grad_sets = jnp.stack(partner_sets(upstream, count_in, link_count, swap_grads))
-    proj_grad = lax.psum(
-        jnp.dot(upstream, right_two[0].T, preferred_element_type=jnp.float32), "tensor"
-    ).astype(jnp.bfloat16)
+    proj_grad = summed(jnp.dot(upstream, right_two[0].T, preferred_element_type=jnp.float32))
     grad_view = grad_sets.reshape(link_count, row_count, count_in, block_size)
     second_view = blocks_two.reshape(count_in, group_size, link_count, block_size, block_size)
     grad_act = jnp.einsum(
@@ -75,9 +71,7 @@
     ).reshape(row_count, hid_count * block_size)
     grad_act = grad_act + jnp.dot(proj_grad, left_two[0].T, preferred_element_type=jnp.float32)
     hidden_grad = (grad_act * slope_vals).astype(jnp.bfloat16)
-    back_rank = lax.psum(
-        jnp.dot(hidden_grad, right_one[0].T, preferred_element_type=jnp.float32), "tensor"
-    ).astype(jnp.bfloat16)
+    back_rank = summed(jnp.dot(hidden_grad, right_one[0].T, preferred_element_type=jnp.float32))
     hidden_view = hidden_grad.reshape(row_count, count_in, group_size, block_size)
     first_view = blocks_one.reshape(count_in, group_size, link_count, block_size, block_size)
     partials = jnp.einsum(

time: 438 us -> 403 us (0.920)
  blocking collectives: 278 us -> 104 us
  waiting for transfers between devices: 51.1 us -> 169 us
  between operations: 0.97 us -> 14 us
  local copies, waits for them, and re-layouts: 30.6 us -> 35.4 us
    psum x2 -> x0, blocking collectives: 278 us -> none  [the longest x1 148 us: body(): lax.psum(jnp.dot(hidden_grad, right_one[0].T, preferred_element_type=jnp....]
    reduce_scatter x0 -> x4, waiting for transfers between devices: none -> 138 us  [summed(): part = lax.psum_scatter(values, 'tensor', scatter_dimension=0, tiled=True)]
    all_gather x0 -> x4, blocking collectives: none -> 104 us  [summed(): lax.all_gather(part.astype(jnp.bfloat16), 'tensor', axis=0, tiled=True)]
    ppermute x15, waiting for transfers between devices: 51.1 us -> 31.2 us  [swapped(): return lax.ppermute(value, axis, pairs)]
    unnamed x54 -> x56, local copies, waits for them, and re-layouts: 26.3 us -> 30.1 us
  transfers between devices with their start and end apart: 16 -> 20, of which waited for: 4 -> 6; matrix products, arithmetic and copies ran while one was open for 10% -> 17% of each run, Pallas kernels for 0% -> 0%
where the time goes in v1:
time: 403 us; the launch traced here: 402 us
  waiting for transfers between devices  169 us (42%)
  blocking collectives  104 us (26%)
  matrix products  47 us (12%)
  local copies, waits for them, and re-layouts  35.4 us (9%)
  starting transfers between devices  26.8 us (7%)
  between operations  14 us (3%)
  other arithmetic  5.36 us (1%)
    reduce_scatter x4, waiting for transfers between devices, summed(): part = lax.psum_scatter(values, 'tensor', scatter_dimension=0, tiled=True)  138 us
    all_gather x4, blocking collectives, summed(): lax.all_gather(part.astype(jnp.bfloat16), 'tensor', axis=0, tiled=True)  104 us
    ppermute x15, waiting for transfers between devices, swapped(): return lax.ppermute(value, axis, pairs)  31.2 us
    unnamed x56, local copies, waits for them, and re-layouts  30.1 us
    ppermute x15, starting transfers between devices, swapped(): return lax.ppermute(value, axis, pairs)  23.3 us
    dot_general x1, matrix products, body(): jnp.einsum('ktcb,cjkeb->tcje', grad_view, second_view, preferred_element_...  8.25 us
  transfers between devices with their start and end apart: 20, of which 6 were waited for; matrix products, arithmetic and copies ran while one was open for 17% of the time, Pallas kernels for 0%

profile of v1, /device:TPU:1, one launch (start us, length us, event | category | flops | bytes accessed | tf_op | source)
XLA Modules:
  0.0 402.1 jit_solution(15232786697021873415)
XLA Ops:
  7.2 2.5 fusion.58
  9.8 0.0 reduce-scatter.11.cloned.1.call-start
  9.8 3.9 copy.16
  13.8 2.3 fusion.17
  16.1 1.3 copy-done.7
  17.4 1.7 fusion.33
  19.2 0.0 reduce-scatter.5.cloned.1.call-start
  19.2 3.4 collective-permute-start
  22.6 3.6 collective-permute-start.15
  26.2 0.7 collective-permute-start.14
  26.9 2.9 collective-permute-start.13
  29.8 1.8 collective-permute-start.11
  31.6 1.9 constant_dynamic-update-slice_fusion
  33.5 1.3 collective-permute-start.12
  34.8 1.3 fusion.61
  36.2 1.1 bitcast_dynamic-update-slice_fusion.10
  37.4 3.7 collective-permute-start.5
  41.1 1.9 bitcast_dynamic-update-slice_fusion.4
  42.9 9.3 %collective-permute-done.12 = bf16[1024,256]{1,0:T(8,128)(2,1)} collective-permute-done((bf16[1024,256]{1,0:T(8,128)(2,1)}, bf16[1024,256]{1,0:T(8,128)(2,1)}, u32[]{:S(2)}, u32[]{:S(2)}) %collective-permute-start.12) | collective-permute-done | bytes 524320 | tf_op jit(solution)/shard_map/ppermute | solution.py:10
  52.3 0.7 collective-permute-start.4
  53.0 1.9 bitcast_dynamic-update-slice_fusion.3
  54.9 2.6 collective-permute-start.1
  57.6 1.9 bitcast_dynamic-update-slice_fusion.2
  59.5 1.1 collective-permute-start.2
  60.6 1.9 bitcast_dynamic-update-slice_fusion.1
  62.5 0.5 collective-permute-start.3
  63.0 2.0 bitcast_dynamic-update-slice_fusion
  65.0 9.7 %collective-permute-done.2 = bf16[1024,256]{1,0:T(8,128)(2,1)S(1)} collective-permute-done((bf16[1024,256]{1,0:T(8,128)(2,1)S(1)}, bf16[1024,256]{1,0:T(8,128)(2,1)S(1)}, u32[]{:S(2)}, u32[]{:S(2)}) %collective-permute-start.2) | collective-permute-done | bytes 524320 | tf_op jit(solution)/shard_map/ppermute | solution.py:10
  74.7 12.1 %collective-permute-done.3 = bf16[1024,256]{1,0:T(8,128)(2,1)S(1)} collective-permute-done((bf16[1024,256]{1,0:T(8,128)(2,1)S(1)}, bf16[1024,256]{1,0:T(8,128)(2,1)S(1)}, u32[]{:S(2)}, u32[]{:S(2)}) %collective-permute-start.3) | collective-permute-done | bytes 524320 | tf_op jit(solution)/shard_map/ppermute | solution.py:10
  87.0 1.7 copy-done.18
  88.7 4.9 %convert_bitcast_fusion.1 = bf16[1,4,6,256,256]{3,4,1,2,0:T(8,128)(2,1)} fusion(bf16[1024,4,256,1]{0,2,1,3:T(8,128)(2,1)S(1)} %bitcast.207, bf16[6,1024,256]{2,1,0:T(8,128)(2,1)S(1)} %bitcast_dynamic-update-slice_fusion.5), kind=kOutput, calls=%fused_computation.31 | convolution fusion | flops 3222798336 | bytes 8388608 | tf_op jit(solution)/shard_map/tcje,ktcb->cjkeb/dot_general | solution.py:95
  93.6 4.6 %copy.27 = bf16[1,4,6,256,256]{4,3,2,1,0:T(8,128)(2,1)} copy(bf16[1,4,6,256,256]{3,4,1,2,0:T(8,128)(2,1)} %convert_bitcast_fusion.1) | data formatting | bytes 6291456
  98.2 8.3 %fusion.24 = f32[1024,4,256,1]{0,2,3,1:T(8,128)} fusion(bf16[1,4,6,256,256]{4,3,2,1,0:T(8,128)(2,1)} %param.13, bf16[6,1024,256]{2,1,0:T(8,128)(2,1)} %copy-done.18), kind=kOutput, calls=%fused_computation.28 | convolution fusion | flops 3221225472 | bytes 10485760 | tf_op jit(solution)/shard_map/ktcb,cjkeb->tcje/dot_general | solution.py:69
  106.5 0.8 convert_element_type.95
  107.2 64.5 %reduce-scatter.11.cloned.1.call-done = f32[32,256]{1,0:T(8,128)} async-done(((f32[1024,256]{1,0:T(8,128)}), f32[32,256]{1,0:T(8,128)}) %reduce-scatter.11.cloned.1.call-update) | async-done | bytes 32784 | tf_op jit(solution)/shard_map/reduce_scatter | solution.py:19
  171.7 0.8 convert_element_type.100
  172.5 28.7 %all_gather.14 = bf16[1024,256]{1,0:T(8,128)(2,1)} all-gather(bf16[32,256]{1,0:T(8,128)(2,1)S(1)} %convert_element_type.95), channel_id=1, replica_groups=mesh['section'=4,'tensor'=32] {'tensor'}, dimensions={0}, use_global_device_ids=true | all-gather | bytes 540672 | tf_op jit(solution)/shard_map/all_gather | solution.py:20
  201.2 22.7 %all_gather.15 = bf16[1024,256]{1,0:T(8,128)(2,1)S(1)} all-gather(bf16[32,256]{1,0:T(8,128)(2,1)S(1)} %convert_element_type.100), channel_id=1, replica_groups=mesh['section'=4,'tensor'=32] {'tensor'}, dimensions={0}, use_global_device_ids=true | all-gather | bytes 540672 | tf_op jit(solution)/shard_map/all_gather | solution.py:20
  223.9 2.1 fusion.50
  226.0 26.5 %reduce-scatter.5.cloned.1.call-done = f32[32,256]{1,0:T(8,128)} async-done(((f32[1024,256]{1,0:T(8,128)}), f32[32,256]{1,0:T(8,128)}) %reduce-scatter.5.cloned.1.call-update) | async-done | bytes 32784 | tf_op jit(solution)/shard_map/reduce_scatter | solution.py:19
  252.5 0.8 convert_element_type.78
  253.3 26.5 %all_gather.12 = bf16[1024,256]{1,0:T(8,128)(2,1)S(1)} all-gather(bf16[32,256]{1,0:T(8,128)(2,1)S(1)} %convert_element_type.78), channel_id=1, replica_groups=mesh['section'=4,'tensor'=32] {'tensor'}, dimensions={0}, use_global_device_ids=true | all-gather | bytes 540672 | tf_op jit(solution)/shard_map/all_gather | solution.py:20
  279.8 4.5 %fusion.12 = bf16[1024,1024]{0,1:T(8,128)(2,1)S(1)} fusion(bf16[1,1024,1024]{1,2,0:T(8,128)(2,1)} %copy.16, f32[1024,4,256,1]{0,2,3,1:T(8,128)} %fusion.24, bf16[1024,256]{1,0:T(8,128)(2,1)S(1)} %all_gather.12, bf16[1,1024,256]{2,1,0:T(8,128)(2,1)} %param.16), kind=kOutput, calls=%fused_computation.15 | convolution fusion | flops 549453824 | bytes 9437184 | tf_op jit(solution)/shard_map/dot_general | solution.py:72
  284.3 1.4 copy-done.4
  285.7 1.7 fusion.51
  287.4 5.1 %fusion.22 = f32[1024,6,256,1]{2,0,1,3:T(8,128)S(1)} fusion(bf16[1024,4,256,1]{0,2,3,1:T(8,128)(2,1)} %bitcast.205, bf16[1,4,6,256,256]{4,3,2,1,0:T(8,128)(2,1)S(1)} %copy-done), kind=kOutput, calls=%fused_computation.26 | convolution fusion | flops 3221225472 | bytes 11534336 | tf_op jit(solution)/shard_map/tcje,cjkbe->ktcb/dot_general | solution.py:77
  292.5 1.1 slice_bitcast_fusion
  293.7 1.2 collective-permute-start.10
  294.8 2.1 slice_bitcast_fusion.4
  296.9 0.1 copy-done.3
  297.0 0.5 collective-permute-start.6
  297.5 2.2 collective-permute-start.8
  299.8 0.4 collective-permute-start.7
  300.2 4.9 %convert_bitcast_fusion.2 = bf16[1,4,6,256,256]{3,4,2,1,0:T(8,128)(2,1)} fusion(bf16[1024,4,256,1]{0,2,3,1:T(8,128)(2,1)S(1)} %bitcast.206, bf16[6,1024,256]{2,1,0:T(8,128)(2,1)S(1)} %copy-done.19), kind=kOutput, calls=%fused_computation.32 | convolution fusion | flops 3222798336 | bytes 8388608 | tf_op jit(solution)/shard_map/ktcb,tcje->cjkbe/dot_general | solution.py:88
  305.1 4.7 %copy.26 = bf16[1,4,6,256,256]{4,3,2,1,0:T(8,128)(2,1)} copy(bf16[1,4,6,256,256]{3,4,2,1,0:T(8,128)(2,1)} %convert_bitcast_fusion.2) | data formatting | bytes 6291456
  309.8 3.3 fusion.44
  313.1 2.0 fusion.45
  315.1 47.0 %reduce-scatter.7.cloned.1.call-done = f32[32,256]{1,0:T(8,128)} async-done(((f32[1024,256]{1,0:T(8,128)}), f32[32,256]{1,0:T(8,128)}) %reduce-scatter.7.cloned.1.call-update) | async-done | bytes 32784 | tf_op jit(solution)/shard_map/reduce_scatter | solution.py:19
  362.1 0.8 convert_element_type.82
  362.8 26.3 %all_gather.13 = bf16[1024,256]{1,0:T(8,128)(2,1)S(1)} all-gather(bf16[32,256]{1,0:T(8,128)(2,1)S(1)} %convert_element_type.82), channel_id=1, replica_groups=mesh['section'=4,'tensor'=32] {'tensor'}, dimensions={0}, use_global_device_ids=true | all-gather | bytes 540672 | tf_op jit(solution)/shard_map/all_gather | solution.py:20
  389.2 0.8 copy-done.6
  390.0 0.3 fusion.49
  390.3 0.8 copy.28
  391.1 4.4 %fusion.48 = bf16[1,1024,256]{2,1,0:T(8,128)(2,1)} fusion(f32[1024,256]{1,0:T(8,128)} %collective-permute-done.10, f32[1024,256]{1,0:T(8,128)} %collective-permute-done.9, f32[1024,256]{1,0:T(8,128)} %collective-permute-done.8, f32[1024,256]{1,0:T(8,128)} %collective-permute-done.7, f32[1024,256]{1,0:T(8,128)} %collective-permute-done.6, ...), kind=kOutput, calls=%fused_computation.47 | convolution fusion | flops 136052736 | bytes 7471104 | tf_op jit(solution)/shard_map/dot_general | solution.py:80
  (63 shorter events, 0.4 us)
Async XLA Ops:
  7.2 280.3 %copy-start = (bf16[1,4,6,256,256]{4,3,2,1,0:T(8,128)(2,1)S(1)}, bf16[1,4,6,256,256]{4,3,2,1,0:T(8,128)(2,1)}, u32[]{:S(2)}) copy-start(bf16[1,4,6,256,256]{4,3,2,1,0:T(8,128)(2,1)} %param.12) | copy-start | bytes 9437188
  7.2 99.3 %reduce-scatter.9.cloned.1.call-start = ((), (), s32[]{:S(2)}) async-start(), calls=%async_computation.6 | async-start | bytes 1081344 | tf_op jit(solution)/shard_map/reduce_scatter | solution.py:19
  9.8 161.9 %reduce-scatter.11.cloned.1.call-start = ((), (), s32[]{:S(2)}) async-start(), calls=%async_computation.7 | async-start | bytes 1081344 | tf_op jit(solution)/shard_map/reduce_scatter | solution.py:19
  13.8 3.6 copy-start.20
  16.1 1.3 copy-start.7
  17.4 17.4 %copy-start.17 = (bf16[1,256,256]{2,1,0:T(8,128)(2,1)S(1)}, bf16[1,256,256]{2,1,0:T(8,128)(2,1)}, u32[]{:S(2)}) copy-start(bf16[1,256,256]{2,1,0:T(8,128)(2,1)} %param.17) | copy-start | bytes 393220
  19.2 233.3 %reduce-scatter.5.cloned.1.call-start = ((), (), s32[]{:S(2)}) async-start(), calls=%async_computation.4 | async-start | bytes 1081344 | tf_op jit(solution)/shard_map/reduce_scatter | solution.py:19
  19.2 14.3 %collective-permute-start = (bf16[1024,256]{1,0:T(8,128)(2,1)}, bf16[1024,256]{1,0:T(8,128)(2,1)S(1)}, u32[]{:S(2)}, u32[]{:S(2)}) collective-permute-start(bf16[1024,256]{1,0:T(8,128)(2,1)} %bitcast.213), channel_id=1, source_target_pairs={{0,96},{32,0},{64,32},{96,64},{1,97},{33,1},{65,33},{97,65},{2,98}... | collective-permute-start | bytes 1572872 | tf_op jit(solution)/shard_map/ppermute | solution.py:15
  22.6 39.9 %collective-permute-start.15 = (bf16[1024,256]{1,0:T(8,128)(2,1)}, bf16[1024,256]{1,0:T(8,128)(2,1)}, u32[]{:S(2)}, u32[]{:S(2)}) collective-permute-start(bf16[1024,256]{1,0:T(8,128)(2,1)} %bitcast.208), channel_id=1, source_target_pairs={{0,16},{1,17},{2,18},{3,19},{4,20},{5,21},{6,22},{7,23},{8,24},{9,... | collective-permute-start | bytes 1572872 | tf_op jit(solution)/shard_map/ppermute | solution.py:10
  26.2 33.3 %collective-permute-start.14 = (bf16[1024,256]{1,0:T(8,128)(2,1)}, bf16[1024,256]{1,0:T(8,128)(2,1)}, u32[]{:S(2)}, u32[]{:S(2)}) collective-permute-start(bf16[1024,256]{1,0:T(8,128)(2,1)} %bitcast.209), channel_id=1, source_target_pairs={{0,8},{1,9},{2,10},{3,11},{4,12},{5,13},{6,14},{7,15},{8,0},{9,1},... | collective-permute-start | bytes 1572872 | tf_op jit(solution)/shard_map/ppermute | solution.py:10
  26.9 28.0 %collective-permute-start.13 = (bf16[1024,256]{1,0:T(8,128)(2,1)}, bf16[1024,256]{1,0:T(8,128)(2,1)}, u32[]{:S(2)}, u32[]{:S(2)}) collective-permute-start(bf16[1024,256]{1,0:T(8,128)(2,1)} %bitcast.210), channel_id=1, source_target_pairs={{0,4},{1,5},{2,6},{3,7},{4,0},{5,1},{6,2},{7,3},{8,12},{9,13},{10,... | collective-permute-start | bytes 1572872 | tf_op jit(solution)/shard_map/ppermute | solution.py:10
  29.8 7.6 %collective-permute-start.11 = (bf16[1024,256]{1,0:T(8,128)(2,1)}, bf16[1024,256]{1,0:T(8,128)(2,1)}, u32[]{:S(2)}, u32[]{:S(2)}) collective-permute-start(bf16[1024,256]{1,0:T(8,128)(2,1)} %bitcast.211), channel_id=1, source_target_pairs={{0,1},{1,0},{2,3},{3,2},{4,5},{5,4},{6,7},{7,6},{8,9},{9,8},{10,11... | collective-permute-start | bytes 1572872 | tf_op jit(solution)/shard_map/ppermute | solution.py:10
  33.5 1.3 copy-start.10
  33.5 18.7 %collective-permute-start.12 = (bf16[1024,256]{1,0:T(8,128)(2,1)}, bf16[1024,256]{1,0:T(8,128)(2,1)}, u32[]{:S(2)}, u32[]{:S(2)}) collective-permute-start(bf16[1024,256]{1,0:T(8,128)(2,1)} %bitcast.212), channel_id=1, source_target_pairs={{0,2},{1,3},{2,0},{3,1},{4,6},{5,7},{6,4},{7,5},{8,10},{9,11},{10,... | collective-permute-start | bytes 1572872 | tf_op jit(solution)/shard_map/ppermute | solution.py:10
  36.2 325.9 %reduce-scatter.7.cloned.1.call-start = ((), (), s32[]{:S(2)}) async-start(), calls=%async_computation.5 | async-start | bytes 1081344 | tf_op jit(solution)/shard_map/reduce_scatter | solution.py:19
  36.2 18.7 %copy-start.11 = (bf16[1024,256]{1,0:T(8,128)(2,1)S(1)}, bf16[1024,256]{1,0:T(8,128)(2,1)}, u32[]{:S(2)}) copy-start(bf16[1024,256]{1,0:T(8,128)(2,1)} %copy-done.10) | copy-start | bytes 1572868
  37.4 49.6 %collective-permute-start.5 = (bf16[1024,256]{1,0:T(8,128)(2,1)}, bf16[1024,256]{1,0:T(8,128)(2,1)S(1)}, u32[]{:S(2)}, u32[]{:S(2)}) collective-permute-start(bf16[1024,256]{1,0:T(8,128)(2,1)} %copy-done.10), channel_id=1, source_target_pairs={{0,16},{1,17},{2,18},{3,19},{4,20},{5,21},{6,22},{7,23},{8,24},{9,... | collective-permute-start | bytes 1572872 | tf_op jit(solution)/shard_map/ppermute | solution.py:10
  52.3 34.6 %collective-permute-start.4 = (bf16[1024,256]{1,0:T(8,128)(2,1)}, bf16[1024,256]{1,0:T(8,128)(2,1)S(1)}, u32[]{:S(2)}, u32[]{:S(2)}) collective-permute-start(bf16[1024,256]{1,0:T(8,128)(2,1)} %copy-done.10), channel_id=1, source_target_pairs={{0,8},{1,9},{2,10},{3,11},{4,12},{5,13},{6,14},{7,15},{8,0},{9,1},... | collective-permute-start | bytes 1572872 | tf_op jit(solution)/shard_map/ppermute | solution.py:10
  54.9 10.0 %collective-permute-start.1 = (bf16[1024,256]{1,0:T(8,128)(2,1)S(1)}, bf16[1024,256]{1,0:T(8,128)(2,1)S(1)}, u32[]{:S(2)}, u32[]{:S(2)}) collective-permute-start(bf16[1024,256]{1,0:T(8,128)(2,1)S(1)} %copy-done.11), channel_id=1, source_target_pairs={{0,1},{1,0},{2,3},{3,2},{4,5},{5,4},{6,7},{7,6},{8,9},{9,8},{10,11... | collective-permute-start | bytes 1572872 | tf_op jit(solution)/shard_map/ppermute | solution.py:10
  59.5 15.2 %collective-permute-start.2 = (bf16[1024,256]{1,0:T(8,128)(2,1)S(1)}, bf16[1024,256]{1,0:T(8,128)(2,1)S(1)}, u32[]{:S(2)}, u32[]{:S(2)}) collective-permute-start(bf16[1024,256]{1,0:T(8,128)(2,1)S(1)} %copy-done.11), channel_id=1, source_target_pairs={{0,2},{1,3},{2,0},{3,1},{4,6},{5,7},{6,4},{7,5},{8,10},{9,11},{10,... | collective-permute-start | bytes 1572872 | tf_op jit(solution)/shard_map/ppermute | solution.py:10
  62.5 26.2 %copy-start.8 = (bf16[1,1024,1024]{1,2,0:T(8,128)(2,1)S(1)}, bf16[1,1024,1024]{1,2,0:T(8,128)(2,1)}, u32[]{:S(2)}) copy-start(bf16[1,1024,1024]{1,2,0:T(8,128)(2,1)} %copy-done.7) | copy-start | bytes 6291460
  62.5 24.4 %collective-permute-start.3 = (bf16[1024,256]{1,0:T(8,128)(2,1)S(1)}, bf16[1024,256]{1,0:T(8,128)(2,1)S(1)}, u32[]{:S(2)}, u32[]{:S(2)}) collective-permute-start(bf16[1024,256]{1,0:T(8,128)(2,1)S(1)} %copy-done.11), channel_id=1, source_target_pairs={{0,4},{1,5},{2,6},{3,7},{4,0},{5,1},{6,2},{7,3},{8,12},{9,13},{10,... | collective-permute-start | bytes 1572872 | tf_op jit(solution)/shard_map/ppermute | solution.py:10
  87.0 1.7 copy-start.18
  279.8 4.5 %copy-start.15 = (bf16[1024,256]{1,0:T(8,128)(2,1)}, bf16[1024,256]{1,0:T(8,128)(2,1)S(1)}, u32[]{:S(2)}) copy-start(bf16[1024,256]{1,0:T(8,128)(2,1)S(1)} %all_gather.12) | copy-start | bytes 1572868
  279.8 5.9 %copy-start.13 = (bf16[1,256,1024]{2,1,0:T(8,128)(2,1)S(1)}, bf16[1,256,1024]{2,1,0:T(8,128)(2,1)}, u32[]{:S(2)}) copy-start(bf16[1,256,1024]{2,1,0:T(8,128)(2,1)} %param.15) | copy-start | bytes 1572868
  284.3 1.4 copy-start.4
  292.5 4.5 %copy-start.3 = (f32[1024,6,256,1]{2,0,1,3:T(8,128)}, f32[1024,6,256,1]{2,0,1,3:T(8,128)S(1)}, u32[]{:S(2)}) copy-start(f32[1024,6,256,1]{2,0,1,3:T(8,128)S(1)} %fusion.22) | copy-start | bytes 18874372
  293.7 97.4 %collective-permute-start.10 = (f32[1024,256]{1,0:T(8,128)}, f32[1024,256]{1,0:T(8,128)}, u32[]{:S(2)}, u32[]{:S(2)}) collective-permute-start(f32[1024,256]{1,0:T(8,128)} %slice_bitcast_fusion), channel_id=1, source_target_pairs={{0,16},{1,17},{2,18},{3,19},{4,20},{5,21},{6,22},{7,23},{8,24},{9,... | collective-permute-start | bytes 3145736 | tf_op jit(solution)/shard_map/ppermute | solution.py:10
  294.8 5.3 %copy-start.5 = (bf16[1024,1024]{0,1:T(8,128)(2,1)S(1)}, bf16[1024,1024]{0,1:T(8,128)(2,1)}, u32[]{:S(2)}) copy-start(bf16[1024,1024]{0,1:T(8,128)(2,1)} %copy-done.4) | copy-start | bytes 6291460
  294.8 5.3 %copy-start.19 = (bf16[6,1024,256]{2,1,0:T(8,128)(2,1)S(1)}, bf16[6,1024,256]{2,1,0:T(8,128)(2,1)}, u32[]{:S(2)}) copy-start(bf16[6,1024,256]{2,1,0:T(8,128)(2,1)} %bitcast_dynamic-update-slice_fusion) | copy-start | bytes 9437188
  297.0 94.1 %collective-permute-start.6 = (f32[1024,256]{1,0:T(8,128)}, f32[1024,256]{1,0:T(8,128)}, u32[]{:S(2)}, u32[]{:S(2)}) collective-permute-start(f32[1024,256]{1,0:T(8,128)} %get-tuple-element.14), channel_id=1, source_target_pairs={{0,1},{1,0},{2,3},{3,2},{4,5},{5,4},{6,7},{7,6},{8,9},{9,8},{10,11... | collective-permute-start | bytes 3145736 | tf_op jit(solution)/shard_map/ppermute | solution.py:10
  297.5 93.6 %collective-permute-start.9 = (f32[1024,256]{1,0:T(8,128)}, f32[1024,256]{1,0:T(8,128)}, u32[]{:S(2)}, u32[]{:S(2)}) collective-permute-start(f32[1024,256]{1,0:T(8,128)} %get-tuple-element.15), channel_id=1, source_target_pairs={{0,8},{1,9},{2,10},{3,11},{4,12},{5,13},{6,14},{7,15},{8,0},{9,1},... | collective-permute-start | bytes 3145736 | tf_op jit(solution)/shard_map/ppermute | solution.py:10
  297.5 93.6 %collective-permute-start.8 = (f32[1024,256]{1,0:T(8,128)}, f32[1024,256]{1,0:T(8,128)}, u32[]{:S(2)}, u32[]{:S(2)}) collective-permute-start(f32[1024,256]{1,0:T(8,128)} %get-tuple-element.16), channel_id=1, source_target_pairs={{0,4},{1,5},{2,6},{3,7},{4,0},{5,1},{6,2},{7,3},{8,12},{9,13},{10,... | collective-permute-start | bytes 3145736 | tf_op jit(solution)/shard_map/ppermute | solution.py:10
  299.8 91.4 %collective-permute-start.7 = (f32[1024,256]{1,0:T(8,128)}, f32[1024,256]{1,0:T(8,128)}, u32[]{:S(2)}, u32[]{:S(2)}) collective-permute-start(f32[1024,256]{1,0:T(8,128)} %get-tuple-element.17), channel_id=1, source_target_pairs={{0,2},{1,3},{2,0},{3,1},{4,6},{5,7},{6,4},{7,5},{8,10},{9,11},{10,... | collective-permute-start | bytes 3145736 | tf_op jit(solution)/shard_map/ppermute | solution.py:10
  305.1 4.7 %copy-start.14 = (bf16[1024,256]{1,0:T(8,128)(2,1)S(1)}, bf16[1024,256]{1,0:T(8,128)(2,1)}, u32[]{:S(2)}) copy-start(bf16[1024,256]{1,0:T(8,128)(2,1)} %all_gather.14) | copy-start | bytes 1572868
  309.8 3.3 copy-start.2
  309.8 3.3 copy-start.16
  313.1 76.9 %copy-start.9 = (bf16[1,1024,256]{2,1,0:T(8,128)(2,1)S(1)}, bf16[1,1024,256]{2,1,0:T(8,128)(2,1)}, u32[]{:S(2)}) copy-start(bf16[1,1024,256]{2,1,0:T(8,128)(2,1)} %param.9) | copy-start | bytes 1572868
  313.1 78.0 %copy-start.12 = (bf16[1,256,256]{2,1,0:T(8,128)(2,1)S(1)}, bf16[1,256,256]{2,1,0:T(8,128)(2,1)}, u32[]{:S(2)}) copy-start(bf16[1,256,256]{2,1,0:T(8,128)(2,1)} %param.14) | copy-start | bytes 393220
  389.2 0.8 copy-start.6
  390.3 5.2 %copy-start.1 = (bf16[1,4,6,256,256]{4,3,2,1,0:T(8,128)(2,1)S(1)}, bf16[1,4,6,256,256]{4,3,2,1,0:T(8,128)(2,1)}, u32[]{:S(2)}) copy-start(bf16[1,4,6,256,256]{4,3,2,1,0:T(8,128)(2,1)} %param.12) | copy-start | bytes 9437188
Sparse Core Ops, SparseCore 0:
  11.5 80.9 reduce-scatter.8
  96.0 75.7 reduce-scatter.10
  175.2 77.2 reduce-scatter.4
  287.6 74.4 reduce-scatter.6

commit v2 on v1

v2 whole, which is shorter than its diff:
```python
import itertools

import jax
import jax.numpy as jnp
from jax import lax
from jax.experimental import pallas as pl
from jax.experimental.pallas import tpu as pltpu
from jax.sharding import PartitionSpec as P

MESH = pl.DeviceIdType.MESH
F32 = jnp.float32
BF16 = jnp.bfloat16
NT = (((1,), (1,)), ((), ()))
CHUNKS = 4
MASKS = {"c": (1,), "y": (2, 4, 6), "z": (8, 16, 24)}


def nt(a, b):
    return lax.dot_general(a, b, NT, preferred_element_type=F32)


def nn(a, b):
    return jnp.dot(a, b, preferred_element_type=F32)


def at(start, size):
    return pl.ds(pl.multiple_of(start, size), size)


def flipped(index, mask):
    result = index
    for bit in range(5):
        if mask >> bit & 1:
            weight = 1 << bit
            result = result + weight * (1 - 2 * ((index // weight) % 2))
    return result


def kernel(
    x_h, pre_h, hand_h, fb_h, sb_h, l1_h, r1_h, l2_h, r2_h,
    ig_o, fg_o, sg_o, l1_o, r1_o, l2_o, r2_o,
    xin, xt, u, act, act_t, slope, ga, w1, w2, hid, l1, r2, paf, br,
    p_out, p_in, sg, fg, ig, l1g, r1g, l2g, r2g,
    pg_ar, pa_ar, br_ar, ssem, rsem, lsem,
):
    tokens = xin.shape[0]
    width = tokens // CHUNKS
    me = lax.axis_index("tensor")
    sec = lax.axis_index("section")
    core, row, col = me % 2, (me // 2) % 4, me // 8
    place = {"c": core, "y": row, "z": col}
    step_of = {"c": 1, "y": 2, "z": 8}
    peer = {m: {"tensor": flipped(me, m)} for m in (1, 2, 4, 6, 8, 16, 24)}
    before, after = {"section": (sec + 3) % 4}, {"section": (sec + 1) % 4}
    numbers, locals_ = itertools.count(), itertools.count()
    sends, stores = [], []

    def send(src, dst, to):
        n = next(numbers)
        copy = pltpu.make_async_remote_copy(
            src_ref=src, dst_ref=dst, send_sem=ssem.at[n], recv_sem=rsem.at[n],
            device_id=to, device_id_type=MESH,
        )
        copy.start()
        sends.append(copy)
        return copy

    def local(src, dst):
        copy = pltpu.make_async_copy(src, dst, lsem.at[next(locals_)])
        copy.start()
        return copy

    def rows(c):
        return pl.ds(c * width, width)

    in_x = local(x_h, xin)
    in_pre = [local(pre_h.at[rows(c)], act.at[rows(c)]) for c in range(CHUNKS)]
    in_small = [local(l1_h, l1), local(r2_h, r2), local(l2_h, w2.at[6])]
    in_w2 = [local(sb_h.at[i], w2.at[pl.ds(0, 6), pl.ds(i * 256, 256)]) for i in range(4)]
    in_w1 = [local(fb_h.at[i], w1.at[pl.ds(0, 6), :, pl.ds(i * 256, 256)]) for i in range(4)]
    in_w1.append(local(r1_h, w1.at[6]))

    barrier = pltpu.get_barrier_semaphore()
    greeted = [*peer.values(), before, after]
    for to in greeted:
        pl.semaphore_signal(barrier, inc=1, device_id=to, device_id_type=MESH)
    pl.semaphore_wait(barrier, len(greeted))

    up0 = [send(hand_h.at[rows(c)], u.at[0, rows(c)], before) for c in range(CHUNKS)]

    in_x.wait()
    halves = [pl.ds(h * 128, 128) for h in range(2)]
    x1, x2, x4, x3, x5 = [], [], [], [], []
    for h in halves:
        xt[0, h, :] = xin[:, h].T
        x2.append(send(xt.at[0, h], xt.at[2, h], peer[2]))
        x4.append(send(xt.at[0, h], xt.at[4, h], peer[8]))
        x1.append(send(xt.at[0, h], xt.at[1, h], peer[1]))

    def pass_inputs(n):
        x2[n].wait_recv()
        x3.append(send(xt.at[2, halves[n]], xt.at[3, halves[n]], peer[6]))
        x4[n].wait_recv()
        x5.append(send(xt.at[4, halves[n]], xt.at[5, halves[n]], peer[24]))

    def summing(bufs, total, order):
        part, part_b, got1, s1, s1_b, got2, s2, s2_b, got3 = bufs
        size = part.shape[0]
        half, quarter, piece = size // 2, size // 8, size // 32
        second, third = order
        base1 = core * half
        base2 = base1 + place[second] * quarter
        base3 = base2 + place[third] * piece

        other = (1 - core) * half
        copy = send(part_b.at[at(other, half)], got1, peer[1])
        yield
        copy.wait_recv()
        s1[...] = part[at(base1, half), :] + got1[...].astype(F32)
        s1_b[...] = s1[...].astype(BF16)
        copies = []
        for n, m in enumerate(MASKS[second]):
            spot = (flipped(me, m) // step_of[second]) % 4
            copies.append(send(s1_b.at[at(spot * quarter, quarter)], got2.at[n], peer[m]))
        yield
        for copy in copies:
            copy.wait_recv()
        mine = s1[at(place[second] * quarter, quarter), :]
        s2[...] = mine + got2[0].astype(F32) + got2[1].astype(F32) + got2[2].astype(F32)
        s2_b[...] = s2[...].astype(BF16)
        copies = []
        for n, m in enumerate(MASKS[third]):
            spot = (flipped(me, m) // step_of[third]) % 4
            copies.append(send(s2_b.at[at(spot * piece, piece)], got3.at[n], peer[m]))
        yield
        for copy in copies:
            copy.wait_recv()
        mine = s2[at(place[third] * piece, piece), :]
        whole = mine + got3[0].astype(F32) + got3[1].astype(F32) + got3[2].astype(F32)
        spot = at(base3, piece)
        total[spot, :] = whole.astype(BF16)
        copies = [send(total.at[spot], total.at[spot], peer[m]) for m in MASKS[third]]
        yield
        for copy in copies:
            copy.wait_recv()
        spot = at(base2, quarter)
        copies = [send(total.at[spot], total.at[spot], peer[m]) for m in MASKS[second]]
        yield
        for copy in copies:
            copy.wait_recv()
        spot = at(base1, half)
        copy = send(total.at[spot], total.at[spot], peer[1])
        yield
        copy.wait_recv()
        yield

    for copy in in_small:
        copy.wait()
    up1, up2, up3, up4, up5 = [], [], [], [], []

    def pass_upstream(c):
        up2[c].wait_recv()
        up3.append(send(u.at[2, rows(c)], u.at[3, rows(c)], peer[6]))
        up4[c].wait_recv()
        up5.append(send(u.at[4, rows(c)], u.at[5, rows(c)], peer[24]))

    for c in range(CHUNKS):
        in_pre[c].wait()

        @pl.loop(0, width // 32)
        def _(r):
            spot = pl.ds(pl.multiple_of(c * width + r * 32, 32), 32)
            for j in range(4):
                lanes = pl.ds(j * 256, 256)
                v = act[spot, lanes].astype(F32)
                cdf = 0.5 * (1.0 + lax.erf(v * 0.7071067811865476))
                density = jnp.exp(-0.5 * v * v) * 0.3989422804014327
                act[spot, lanes] = (v * cdf).astype(BF16)
                slope[spot, lanes] = cdf + v * density

        up0[c].wait_recv()
        up2.append(send(u.at[0, rows(c)], u.at[2, rows(c)], peer[2]))
        up4.append(send(u.at[0, rows(c)], u.at[4, rows(c)], peer[8]))
        up1.append(send(u.at[0, rows(c)], u.at[1, rows(c)], peer[1]))
        value = nt(u[0, rows(c), :], r2[...])
        pg_ar[0][rows(c), :] = value
        pg_ar[1][rows(c), :] = value.astype(BF16)
        if c >= 1:
            pass_upstream(c - 1)
        if c in (1, 2):
            pass_inputs(c - 1)

        @pl.loop(0, 4)
        def _(j):
            act_t[at(j * 256, 256), rows(c)] = act[rows(c), at(j * 256, 256)].T

    pg = summing(pg_ar, u.at[6], ("y", "z"))
    next(pg)
    pass_upstream(CHUNKS - 1)

    left = l1[...].T
    pa_ar[0][pl.ds(0, 256), :] = nn(left, xt[0])
    left = w2[6].T
    pa_ar[0][pl.ds(256, 256), :] = nn(left, act_t[...])
    pa_ar[1][...] = pa_ar[0][...].astype(BF16)
    next(pg)
    pa = summing(pa_ar, paf, ("z", "y"))
    next(pa)

    for copy in in_w2:
        copy.wait()

    def block_terms(c):
        for group in (up1, up2, up3, up4, up5):
            if group is not up2 and group is not up4:
                group[c].wait_recv()
        left = jnp.concatenate([u[k, rows(c), :] for k in range(6)], axis=1)

        @pl.loop(0, 4)
        def _(j):
            block = at(j * 256, 256)
            right = jnp.concatenate([w2[k, block, :] for k in range(6)], axis=1)
            ga[rows(c), block] = nt(left, right)

    def second_terms(first, last):
        @pl.loop(first, last)
        def _(k):
            value = nn(act_t[...], u[k]).astype(BF16)
            for i in range(4):
                sg[i, k] = value[i * 256 : (i + 1) * 256]

    block_terms(0)
    next(pg)
    block_terms(1)
    next(pa)
    block_terms(2)
    next(pg)
    block_terms(3)
    next(pa)
    second_terms(0, 1)
    next(pg)
    second_terms(1, 2)
    next(pa)
    next(pg)
    second_terms(2, 4)
    next(pa)
    next(pg)

    for copy in in_w1:
        copy.wait()
    in1, in2, in4, got2, got4 = [], [], [], [], []

    def merge(c):
        got2[c].wait_recv()
        p_out[1, rows(c), :] = (ga[rows(c), pl.ds(256, 256)] + p_in[3, rows(c), :].astype(F32)).astype(BF16)
        in2.append(send(p_out.at[1, rows(c)], p_in.at[1, rows(c)], peer[2]))
        got4[c].wait_recv()
        p_out[2, rows(c), :] = (ga[rows(c), pl.ds(512, 256)] + p_in[4, rows(c), :].astype(F32)).astype(BF16)
        in4.append(send(p_out.at[2, rows(c)], p_in.at[2, rows(c)], peer[8]))

    for c in range(CHUNKS):

        @pl.loop(0, 4)
        def _(j):
            block = at(j * 256, 256)
            grad = ga[rows(c), block] + nt(u[6, rows(c), :], w2[6, block, :])
            hid[rows(c), block] = (grad * slope[rows(c), block]).astype(BF16)

        h = hid[rows(c), :]
        p_out[3, rows(c), :] = nt(h, w1[3]).astype(BF16)
        got2.append(send(p_out.at[3, rows(c)], p_in.at[3, rows(c)], peer[6]))
        p_out[4, rows(c), :] = nt(h, w1[5]).astype(BF16)
        got4.append(send(p_out.at[4, rows(c)], p_in.at[4, rows(c)], peer[24]))
        p_out[0, rows(c), :] = nt(h, w1[1]).astype(BF16)
        in1.append(send(p_out.at[0, rows(c)], p_in.at[0, rows(c)], peer[1]))
        value = nt(h, w1[6])
        br_ar[0][rows(c), :] = value
        br_ar[1][rows(c), :] = value.astype(BF16)
        ga[rows(c), pl.ds(256, 256)] = nt(h, w1[2])
        ga[rows(c), pl.ds(512, 256)] = nt(h, w1[4])
        ga[rows(c), pl.ds(0, 256)] = nt(h, w1[0])
        if c >= 1:
            merge(c - 1)

    back = summing(br_ar, br, ("y", "z"))
    next(back)
    next(pa)
    second_terms(4, 6)
    stores.append(local(sg, sg_o))
    merge(CHUNKS - 1)
    next(back)
    next(pa)
    for group in (x1, x3, x5):
        for copy in group:
            copy.wait_recv()

    def first_terms(first, last):
        @pl.loop(first, last)
        def _(k):
            for i in range(4):
                block = pl.ds(i * 256, 256)
                fg[i, k] = nn(xt[k], hid[:, block]).astype(BF16)

    first_terms(0, 2)
    next(back)
    first_terms(2, 4)
    next(back)
    first_terms(4, 6)
    stores.append(local(fg, fg_o))
    next(back)
    l2g[...] = nn(act_t[...], u[6]).astype(BF16)
    stores.append(local(l2g, l2_o))
    r1g[...] = nn(paf[pl.ds(0, 256), :], hid[...]).astype(BF16)
    stores.append(local(r1g, r1_o))
    next(back)
    r2g[...] = nn(paf[pl.ds(256, 256), :], u[0]).astype(BF16)
    stores.append(local(r2g, r2_o))
    next(back)
    l1g[...] = nn(xt[0], br[...]).astype(BF16)
    stores.append(local(l1g, l1_o))
    for c in range(CHUNKS):
        value = ga[rows(c), pl.ds(0, 256)] + nt(br[rows(c), :], l1[...])
        for n, group in enumerate((in1, in2, in4)):
            group[c].wait_recv()
            value = value + p_in[n, rows(c), :].astype(F32)
        ig[rows(c), :] = value.astype(BF16)
        stores.append(local(ig.at[rows(c)], ig_o.at[rows(c)]))
    for copy in sends:
        copy.wait_send()
    for copy in stores:
        copy.wait()


def sum_buffers(size, lanes):
    return (
        pltpu.VMEM((size, lanes), F32),
        pltpu.VMEM((size, lanes), BF16),
        pltpu.VMEM((size // 2, lanes), BF16),
        pltpu.VMEM((size // 2, lanes), F32),
        pltpu.VMEM((size // 2, lanes), BF16),
        pltpu.VMEM((3, size // 8, lanes), BF16),
        pltpu.VMEM((size // 8, lanes), F32),
        pltpu.VMEM((size // 8, lanes), BF16),
        pltpu.VMEM((3, size // 32, lanes), BF16),
    )


def body(*args):
    args = [a[0] for a in args]
    x, pre, _, fb, _, l1, r1, l2, r2 = args
    t, b = x.shape
    h = pre.shape[1]
    k = fb.shape[1]
    outs = [x, fb, fb, l1, r1, l2, r2]
    vm = pltpu.VMEM
    scratch = [
        vm((t, b), BF16), vm((k, b, t), BF16), vm((k + 1, t, b), BF16), vm((t, h), BF16),
        vm((h, t), BF16), vm((t, h), F32), vm((t, h), F32), vm((k + 1, b, h), BF16),
        vm((k + 1, h, b), BF16), vm((t, h), BF16), vm((b, b), BF16), vm((b, b), BF16),
        vm((2 * b, t), BF16), vm((t, b), BF16), vm((5, t, b), BF16), vm((5, t, b), BF16),
        vm(fb.shape, BF16), vm(fb.shape, BF16), vm((t, b), BF16), vm((b, b), BF16),
        vm((b, h), BF16), vm((h, b), BF16), vm((b, b), BF16),
        sum_buffers(t, b), sum_buffers(2 * b, t), sum_buffers(t, b),
        pltpu.SemaphoreType.DMA((112,)), pltpu.SemaphoreType.DMA((112,)),
        pltpu.SemaphoreType.DMA((40,)),
    ]
    results = pl.pallas_call(
        kernel,
        out_shape=[jax.ShapeDtypeStruct(o.shape, o.dtype) for o in outs],
        in_specs=[pl.BlockSpec(memory_space=pl.ANY)] * 9,
        out_specs=[pl.BlockSpec(memory_space=pl.ANY)] * 7,
        scratch_shapes=scratch,
        compiler_params=pltpu.CompilerParams(
            collective_id=0, has_side_effects=True, vmem_limit_bytes=62 * 1024 * 1024
        ),
    )(*args)
    return tuple(r[None] for r in results)


def solution(mesh):
    three = P("section", None, "tensor")
    rows = P("section", "tensor", None)
    blocks = P("section", "tensor", None, None, None)
    return jax.shard_map(
        body,
        mesh=mesh,
        in_specs=(three, three, three, blocks, blocks, rows, three, rows, three),
        out_specs=(three, blocks, blocks, rows, three, rows, three),
        check_vma=False,
    )
```

time: 403 us -> 122 us (0.30)
  waiting for transfers between devices: 169 us -> 0 us
  Pallas kernels: 0 us -> 110 us
  blocking collectives: 104 us -> 0 us
  matrix products: 47 us -> 0 us
  starting transfers between devices: 26.8 us -> 0 us
  local copies, waits for them, and re-layouts: 35.4 us -> 10.5 us
  between operations: 14 us -> 0.66 us
  other arithmetic: 5.36 us -> 0 us
    reduce_scatter x4 -> x0, waiting for transfers between devices: 138 us -> none  [summed(): part = lax.psum_scatter(values, 'tensor', scatter_dimension=0, tiled=True)]
    pallas_call x0 -> x1, Pallas kernels: none -> 110 us  [body(): pl.pallas_call(kernel, out_shape=[jax.ShapeDtypeStruct(o.shape, o.dtype)...]
    all_gather x4 -> x0, blocking collectives: 104 us -> none  [summed(): lax.all_gather(part.astype(jnp.bfloat16), 'tensor', axis=0, tiled=True)]
    dot_general x14 -> x0, matrix products: 47 us -> none  [the longest x1 8.25 us: body(): jnp.einsum('ktcb,cjkeb->tcje', grad_view, second_view, preferred_element_...]
    ppermute x16 -> x0, waiting for transfers between devices: 31.2 us -> none  [the longest x15 31.2 us: swapped(): return lax.ppermute(value, axis, pairs)]
    ppermute x16 -> x0, starting transfers between devices: 26.6 us -> none  [the longest x15 23.3 us: swapped(): return lax.ppermute(value, axis, pairs)]
    unnamed x56 -> x17, local copies, waits for them, and re-layouts: 30.1 us -> 10.5 us
    convert_element_type x5 -> x0, other arithmetic: 5.36 us -> none  [the longest x4 3.05 us: summed(): part.astype(jnp.bfloat16)]
  transfers between devices with their start and end apart: 20 -> 0, of which waited for: 6 -> 0; matrix products, arithmetic and copies ran while one was open for 17% -> 0% of each run, Pallas kernels for 0% -> 0%
where the time goes in v2:
time: 122 us; the launch traced here: 121 us
  Pallas kernels  110 us (90%)
  local copies, waits for them, and re-layouts  10.5 us (9%)
    pallas_call x1, Pallas kernels, body(): pl.pallas_call(kernel, out_shape=[jax.ShapeDtypeStruct(o.shape, o.dtype)...  110 us
    unnamed x17, local copies, waits for them, and re-layouts  10.5 us

profile of v2, /device:TPU:1, one launch (start us, length us, event | category | flops | bytes accessed | tf_op | source)
XLA Modules:
  0.0 121.4 jit_solution(17834108273666749782)
XLA Ops:
  0.6 110.3 %shard_map.144 = (bf16[1024,256]{1,0:T(8,128)(2,1)}, bf16[4,6,256,256]{3,2,1,0:T(8,128)(2,1)}, bf16[4,6,256,256]{3,2,1,0:T(8,128)(2,1)}, bf16[256,256]{1,0:T(8,1...) custom-call(bf16[1024,256]{1,0:T(8,128)(2,1)} %bitcast.24, ...), custom_call_target="tpu_custom_call" | custom-call | tf_op jit(solution)/shard_map/pallas_call | solution.py:367
  110.9 1.9 %copy.23 = bf16[1,1024,256]{2,1,0:T(8,128)(2,1)} copy(bf16[1,1024,256]{2,1,0:T(8,128)(2,1)} %bitcast.23) | data formatting | bytes 1048576
  112.8 0.0 copy-start
  112.8 4.0 %copy.24 = bf16[1,4,6,256,256]{4,3,2,1,0:T(8,128)(2,1)} copy(bf16[1,4,6,256,256]{4,3,2,1,0:T(8,128)(2,1)} %bitcast.17) | data formatting | bytes 6291456
  116.8 0.0 copy-done
  116.8 0.0 copy-start.4
  116.8 0.0 copy-start.2
  116.8 0.0 copy-start.1
  116.8 0.0 copy-start.3
  116.8 1.7 %copy.25 = bf16[1,4,6,256,256]{4,3,2,1,0:T(8,128)(2,1)} copy(bf16[1,4,6,256,256]{4,3,2,1,0:T(8,128)(2,1)S(1)} %bitcast.16) | data formatting | bytes 6291456
  118.5 0.0 copy-done.4
  118.5 0.7 copy.26
  119.1 0.0 copy-done.2
  119.1 0.8 copy.27
  119.9 0.0 copy-done.1
  119.9 0.8 copy.28
  120.7 0.0 copy-done.3
  120.7 0.7 copy.29
Async XLA Ops:
  112.8 4.0 %copy-start = (bf16[4,6,256,256]{3,2,1,0:T(8,128)(2,1)S(1)}, bf16[4,6,256,256]{3,2,1,0:T(8,128)(2,1)}, u32[]{:S(2)}) copy-start(bf16[4,6,256,256]{3,2,1,0:T(8,128)(2,1)} %get-tuple-element.16) | copy-start | bytes 9437188
  116.8 1.7 %copy-start.4 = (bf16[256,256]{1,0:T(8,128)(2,1)S(1)}, bf16[256,256]{1,0:T(8,128)(2,1)}, u32[]{:S(2)}) copy-start(bf16[256,256]{1,0:T(8,128)(2,1)} %get-tuple-element.17) | copy-start | bytes 393220
  116.8 2.3 %copy-start.2 = (bf16[256,1024]{1,0:T(8,128)(2,1)S(1)}, bf16[256,1024]{1,0:T(8,128)(2,1)}, u32[]{:S(2)}) copy-start(bf16[256,1024]{1,0:T(8,128)(2,1)} %get-tuple-element.18) | copy-start | bytes 1572868
  116.8 3.1 %copy-start.1 = (bf16[1024,256]{1,0:T(8,128)(2,1)S(1)}, bf16[1024,256]{1,0:T(8,128)(2,1)}, u32[]{:S(2)}) copy-start(bf16[1024,256]{1,0:T(8,128)(2,1)} %get-tuple-element.19) | copy-start | bytes 1572868
  116.8 3.9 %copy-start.3 = (bf16[256,256]{1,0:T(8,128)(2,1)S(1)}, bf16[256,256]{1,0:T(8,128)(2,1)}, u32[]{:S(2)}) copy-start(bf16[256,256]{1,0:T(8,128)(2,1)} %get-tuple-element.20) | copy-start | bytes 393220

commit v3 on v2

v3 whole, which is shorter than its diff:
```python
import itertools

import jax
import jax.numpy as jnp
from jax import lax
from jax.experimental import pallas as pl
from jax.experimental.pallas import tpu as pltpu
from jax.sharding import PartitionSpec as P

MESH = pl.DeviceIdType.MESH
F32 = jnp.float32
BF16 = jnp.bfloat16
NT = (((1,), (1,)), ((), ()))
CHUNKS = 4
MASKS = {"c": (1,), "y": (2, 4, 6), "z": (8, 16, 24)}


def nt(a, b):
    return lax.dot_general(a, b, NT, preferred_element_type=F32)


def nn(a, b):
    return jnp.dot(a, b, preferred_element_type=F32)


def at(start, size):
    return pl.ds(pl.multiple_of(start, size), size)


def flipped(index, mask):
    result = index
    for bit in range(5):
        if mask >> bit & 1:
            weight = 1 << bit
            result = result + weight * (1 - 2 * ((index // weight) % 2))
    return result


def kernel(
    x_h, pre_h, hand_h, fb_h, sb_h, l1_h, r1_h, l2_h, r2_h,
    ig, fg, sg, l1g, r1g, l2g, r2g,
    xin, hand, xt, u, act, act_t, slope, ga, w1, w2, hid, l1, r2, paf, br,
    p_out, p_in, pg_ar, pa_ar, br_ar, ssem, rsem, lsem,
):
    tokens = xin.shape[0]
    width = tokens // CHUNKS
    me = lax.axis_index("tensor")
    sec = lax.axis_index("section")
    core, row, col = me % 2, (me // 2) % 4, me // 8
    peer = {m: {"tensor": flipped(me, m)} for m in (1, 2, 4, 6, 8, 16, 24)}
    before, after = {"section": (sec + 3) % 4}, {"section": (sec + 1) % 4}
    numbers, locals_ = itertools.count(), itertools.count()

    taken = {}

    def spot_of(kind, key):
        return taken.setdefault((kind, key), sum(k == kind for k, _ in taken))

    def send(src, dst, to, name, arrival=None):
        count = next(numbers)
        copy = pltpu.make_async_remote_copy(
            src_ref=src,
            dst_ref=dst,
            send_sem=ssem.at[spot_of("send", name)],
            recv_sem=rsem.at[spot_of("recv", arrival or count)],
            device_id=to,
            device_id_type=MESH,
        )
        copy.start()
        return copy

    def sent(name, ref):
        pltpu.make_async_copy(ref, ref, ssem.at[taken["send", name]]).wait()

    def got(name, ref):
        pltpu.make_async_copy(ref, ref, rsem.at[taken["recv", name]]).wait()

    def local(src, dst, name=None):
        copy = pltpu.make_async_copy(src, dst, lsem.at[spot_of("local", name or next(locals_))])
        copy.start()
        return copy

    def loaded(name, ref):
        pltpu.make_async_copy(ref, ref, lsem.at[taken["local", name]]).wait()

    def rows(c):
        return pl.ds(c * width, width)

    in_hand = local(hand_h, hand)
    in_x = local(x_h, xin)
    in_pre = [local(pre_h.at[rows(c)], act.at[rows(c)]) for c in range(CHUNKS)]
    in_small = [local(l1_h, l1), local(l2_h, w2.at[6])]
    for i in range(4):
        local(sb_h.at[i], w2.at[pl.ds(0, 6), pl.ds(i * 256, 256)], "w2")
    for i in range(4):
        local(fb_h.at[i], w1.at[pl.ds(0, 6), :, pl.ds(i * 256, 256)], "w1")
    local(r1_h, w1.at[6], "w1")

    barrier = pltpu.get_barrier_semaphore()
    greeted = [{"tensor": flipped(me, m)} for m in (1, *range(2, 32, 2))] + [before, after]
    for to in greeted:
        pl.semaphore_signal(barrier, inc=1, device_id=to, device_id_type=MESH)
    pl.semaphore_wait(barrier, len(greeted))

    in_r2 = send(r2_h, r2, after, "r2")
    up0 = [send(hand_h.at[rows(c)], u.at[0, rows(c)], before, "hand") for c in range(CHUNKS)]

    def mixed(a, b):
        return a * (1 - core) + b * core

    flips_y = [flipped(me, m) for m in MASKS["y"]]
    flips_z = [flipped(me, m) for m in MASKS["z"]]
    second_to = [{"tensor": mixed(a, b)} for a, b in zip(flips_y, flips_z)]
    third_to = [{"tensor": mixed(b, a)} for a, b in zip(flips_y, flips_z)]
    second_at = [mixed((a // 2) % 4, b // 8) for a, b in zip(flips_y, flips_z)]
    third_at = [mixed(b // 8, (a // 2) % 4) for a, b in zip(flips_y, flips_z)]
    second_me, third_me = mixed(row, col), mixed(col, row)

    def summing(bufs, total, name):
        part, got1, s1, s1_b, got2, s2, got3, _ = bufs
        size = part.shape[0]
        half, quarter, piece = size // 2, size // 8, size // 32
        base1 = core * half
        base2 = base1 + second_me * quarter
        base3 = base2 + third_me * piece

        send(part.at[at((1 - core) * half, half)], got1, peer[1], name + "1", name + "1")
        yield
        got(name + "1", got1)
        s1[...] = part[at(core * half, half), :] + got1[...]
        s1_b[...] = s1[...].astype(BF16)
        for n in range(3):
            spot = at(second_at[n] * quarter, quarter)
            send(s1_b.at[spot], got2.at[n], second_to[n], name + "2", name + "2")
        yield
        got(name + "2", got2)
        mine = s1[at(second_me * quarter, quarter), :]
        s2[...] = mine + got2[0].astype(F32) + got2[1].astype(F32) + got2[2].astype(F32)
        for n in range(3):
            spot = at(third_at[n] * piece, piece)
            send(s2.at[spot], got3.at[n], third_to[n], name + "3", name + "3")
        yield
        got(name + "3", got3)
        mine = s2[at(third_me * piece, piece), :]
        spot = at(base3, piece)
        total[spot, :] = (mine + got3[0] + got3[1] + got3[2]).astype(BF16)
        for to in third_to:
            send(total.at[spot], total.at[spot], to, name + "4", name + "4")
        yield
        got(name + "4", s1_b.at[pl.ds(0, 3 * piece)])
        spot = at(base2, quarter)
        for to in second_to:
            send(total.at[spot], total.at[spot], to, name + "5", name + "5")
        yield
        got(name + "5", got2)
        spot = at(base1, half)
        send(total.at[spot], total.at[spot], peer[1], name + "6", name + "6")
        yield
        got(name + "6", s1_b)
        yield

    others = [flipped(me, m) for m in range(2, 32, 2)]

    def summing_all(bufs, total, name, ship=False):
        part, got1, s1, s1_b, got2, shipped = bufs
        size = part.shape[0]
        half, piece = size // 2, size // 32
        mine = core * half + (me // 2) * piece

        send(part.at[at((1 - core) * half, half)], got1, peer[1], name + "1", name + "1")
        yield
        got(name + "1", got1)
        s1[...] = part[at(core * half, half), :] + got1[...]
        s1_b[...] = s1[...].astype(BF16)
        for n, to in enumerate(others):
            spot = at((to // 2) * piece, piece)
            send(s1_b.at[spot], got2.at[n], {"tensor": to}, name + "2", name + "2")
        yield
        got(name + "2", got2)
        whole = s1[at((me // 2) * piece, piece), :]
        for n in range(len(others)):
            whole = whole + got2[n].astype(F32)
        spot = at(mine, piece)
        if ship:
            shipped[...] = whole.astype(BF16)
            send(shipped, total.at[spot], before, name + "3", name + "3")
            yield
            got(name + "3", shipped)
        else:
            total[spot, :] = whole.astype(BF16)
        for to in others:
            send(total.at[spot], total.at[spot], {"tensor": to}, name + "4", name + "4")
        yield
        got(name + "4", got2)
        spot = at(core * half, half)
        send(total.at[spot], total.at[spot], peer[1], name + "5", name + "5")
        yield
        got(name + "5", s1_b)
        yield

    def activate(c):
        in_pre[c].wait()

        @pl.loop(0, width // 32)
        def _(r):
            spot = pl.ds(pl.multiple_of(c * width + r * 32, 32), 32)
            for j in range(4):
                lanes = pl.ds(j * 256, 256)
                v = act[spot, lanes].astype(F32)
                cdf = 0.5 * (1.0 + lax.erf(v * 0.7071067811865476))
                density = jnp.exp(-0.5 * v * v) * 0.3989422804014327
                act[spot, lanes] = (v * cdf).astype(BF16)
                slope[spot, lanes] = cdf + v * density

        @pl.loop(0, 4)
        def _(j):
            act_t[at(j * 256, 256), rows(c)] = act[rows(c), at(j * 256, 256)].T

    up2, up3, up4, up5 = [], [], [], []

    def give_upstream(c):
        up0[c].wait_recv()
        up2.append(send(u.at[0, rows(c)], u.at[2, rows(c)], peer[2], "up"))
        up4.append(send(u.at[0, rows(c)], u.at[4, rows(c)], peer[8], "up"))
        send(u.at[0, rows(c)], u.at[1, rows(c)], peer[1], "up", "up1")

    def pass_upstream(c):
        up2[c].wait_recv()
        up3.append(send(u.at[2, rows(c)], u.at[3, rows(c)], peer[6], "up"))
        up4[c].wait_recv()
        up5.append(send(u.at[4, rows(c)], u.at[5, rows(c)], peer[24], "up"))

    x2, x4 = [], []
    parts = [pl.ds(n * 64, 64) for n in range(4)]

    def give_inputs(n):
        x2.append(send(xt.at[0, parts[n]], xt.at[2, parts[n]], peer[2], "in"))
        x4.append(send(xt.at[0, parts[n]], xt.at[4, parts[n]], peer[8], "in"))
        send(xt.at[0, parts[n]], xt.at[1, parts[n]], peer[1], "in", "in")

    def pass_inputs(n):
        x2[n].wait_recv()
        send(xt.at[2, parts[n]], xt.at[3, parts[n]], peer[6], "in", "in")
        x4[n].wait_recv()
        send(xt.at[4, parts[n]], xt.at[5, parts[n]], peer[24], "in", "in")

    def block_terms(c):
        for group in (up3, up5):
            group[c].wait_recv()
        left = jnp.concatenate([u[k, rows(c), :] for k in range(6)], axis=1)

        @pl.loop(0, 4)
        def _(j):
            block = at(j * 256, 256)
            right = jnp.concatenate([w2[k, block, :] for k in range(6)], axis=1)
            ga[rows(c), block] = nt(left, right)

    def second_terms(first, last):
        @pl.loop(first, last)
        def _(k):
            value = nn(act_t[...], u[k]).astype(BF16)
            for i in range(4):
                sg[i, k] = value[i * 256 : (i + 1) * 256]

    in_x.wait()
    for n in range(2):
        xt[0, pl.ds(n * 128, 128), :] = xin[:, pl.ds(n * 128, 128)].T
    give_inputs(0)
    give_inputs(1)
    activate(0)
    activate(1)
    activate(2)
    in_hand.wait()
    in_r2.wait_recv()
    pg_ar[0][...] = nt(hand[...], r2[...])
    pg = summing_all(pg_ar, u.at[6], "pg", ship=True)
    next(pg)
    give_upstream(0)
    activate(3)
    next(pg)
    pass_inputs(0)
    for copy in in_small:
        copy.wait()
    pa_ar[0][pl.ds(0, 256), :] = nn(l1[...].T, xt[0])
    pa_ar[0][pl.ds(256, 256), :] = nn(w2[6].T, act_t[...])
    pa = summing(pa_ar, paf, "pa")
    next(pa)
    give_upstream(1)
    pass_inputs(1)
    pass_upstream(0)
    give_upstream(2)
    give_upstream(3)
    pass_upstream(1)
    second_terms(0, 1)
    give_inputs(2)
    pass_upstream(2)
    next(pg)
    got("up1", u.at[1])
    second_terms(1, 2)
    pass_upstream(3)
    next(pg)
    next(pa)
    give_inputs(3)
    loaded("w2", w2.at[pl.ds(0, 6)])
    block_terms(0)
    block_terms(1)
    pass_inputs(2)
    second_terms(2, 3)
    block_terms(2)
    second_terms(4, 5)
    block_terms(3)
    next(pg)
    second_terms(3, 4)
    pass_inputs(3)
    second_terms(5, 6)
    next(pg)
    next(pa)

    loaded("w1", w1)
    far2, far4 = [], []

    def hidden(c):
        @pl.loop(0, 2)
        def _(j):
            block = at(j * 512, 512)
            grad = ga[rows(c), block] + nt(u[6, rows(c), :], w2[6, block, :])
            hid[rows(c), block] = (grad * slope[rows(c), block]).astype(BF16)

    def both(h):
        return pl.ds(h * 2 * width, 2 * width)

    def far_terms(h):
        p_out[3, both(h), :] = nt(hid[both(h), :], w1[3]).astype(BF16)
        p_out[4, both(h), :] = nt(hid[both(h), :], w1[5]).astype(BF16)

    def far_sends(h):
        for c in (2 * h, 2 * h + 1):
            far2.append(send(p_out.at[3, rows(c)], p_in.at[3, rows(c)], peer[6], "p"))
            far4.append(send(p_out.at[4, rows(c)], p_in.at[4, rows(c)], peer[24], "p"))

    def near_terms(h):
        left = hid[both(h), :]
        p_out[0, both(h), :] = nt(left, w1[1]).astype(BF16)
        for c in (2 * h, 2 * h + 1):
            send(p_out.at[0, rows(c)], p_in.at[0, rows(c)], peer[1], "p", "p")
        ga[both(h), pl.ds(256, 256)] = nt(left, w1[2])
        ga[both(h), pl.ds(512, 256)] = nt(left, w1[4])
        ga[both(h), pl.ds(0, 256)] = nt(left, w1[0])

    def merge(c):
        for n, far, mask in ((1, far2, 2), (2, far4, 8)):
            far[c].wait_recv()
            own = ga[rows(c), pl.ds(256 * n, 256)]
            p_out[n, rows(c), :] = (own + p_in[n + 2, rows(c), :].astype(F32)).astype(BF16)
            send(p_out.at[n, rows(c)], p_in.at[n, rows(c)], peer[mask], "p", "p")

    def first_terms(first, last):
        @pl.loop(first, last)
        def _(k):
            for i in range(4):
                block = pl.ds(i * 256, 256)
                fg[i, k] = nn(xt[k], hid[:, block]).astype(BF16)

    for c in range(CHUNKS):
        hidden(c)
    br_ar[0][...] = nt(hid[...], w1[6])
    back = summing_all(br_ar, br, "br")
    next(back)
    next(pa)
    far_terms(0)
    next(back)
    next(pa)
    far_sends(0)
    near_terms(0)
    far_terms(1)
    far_sends(1)
    near_terms(1)
    got("in", xt.at[pl.ds(0, 3)])
    first_terms(0, 2)
    merge(0)
    next(back)
    first_terms(2, 3)
    merge(1)
    first_terms(3, 4)
    next(pa)
    merge(2)
    first_terms(4, 5)
    merge(3)
    first_terms(5, 6)
    l2g[...] = nn(act_t[...], u[6]).astype(BF16)
    next(back)
    next(pa)
    r1g[...] = nn(paf[pl.ds(0, 256), :], hid[...]).astype(BF16)
    r2g[...] = nn(paf[pl.ds(256, 256), :], u[0]).astype(BF16)
    got("p", p_in.at[pl.ds(0, 3)])
    for c in range(CHUNKS):
        value = ga[rows(c), pl.ds(0, 256)]
        for n in range(3):
            value = value + p_in[n, rows(c), :].astype(F32)
        ga[rows(c), pl.ds(0, 256)] = value
    next(back)
    l1g[...] = nn(xt[0], br[...]).astype(BF16)
    ig[...] = (ga[:, pl.ds(0, 256)] + nt(br[...], l1[...])).astype(BF16)
    sent("r2", r2)
    sent("hand", hand)
    sent("up", u.at[pl.ds(0, 5)])
    sent("in", xt.at[pl.ds(0, 5)])
    sent("p", p_out)
    for name, (part, got1, s1, s1_b, got2, *_) in (("pg", pg_ar), ("br", br_ar)):
        sent(name + "1", got1)
        sent(name + "2", got2)
        if name == "pg":
            sent("pg3", pg_ar[5])
        sent(name + "4", got2)
        sent(name + "5", s1_b)
    part, got1, s1, s1_b, got2, s2, got3, _ = pa_ar
    sent("pa1", got1)
    sent("pa2", got2)
    sent("pa3", got3)
    sent("pa4", s1_b.at[pl.ds(0, 48)])
    sent("pa5", got2)
    sent("pa6", s1_b)


def write_out(*refs):
    count = len(refs) // 2
    sems = refs[-1]
    copies = [pltpu.make_async_copy(refs[n], refs[count + n], sems.at[n]) for n in range(count)]
    for copy in copies:
        copy.start()
    for copy in copies:
        copy.wait()


def sum_buffers(size, lanes):
    return (
        pltpu.VMEM((size, lanes), F32),
        pltpu.VMEM((size // 2, lanes), F32),
        pltpu.VMEM((size // 2, lanes), F32),
        pltpu.VMEM((size // 2, lanes), BF16),
        pltpu.VMEM((3, size // 8, lanes), BF16),
        pltpu.VMEM((size // 8, lanes), F32),
        pltpu.VMEM((3, size // 32, lanes), F32),
        pltpu.VMEM((size // 32, lanes), BF16),
    )


def wide_buffers(size, lanes):
    return (
        pltpu.VMEM((size, lanes), F32),
        pltpu.VMEM((size // 2, lanes), F32),
        pltpu.VMEM((size // 2, lanes), F32),
        pltpu.VMEM((size // 2, lanes), BF16),
        pltpu.VMEM((15, size // 32, lanes), BF16),
        pltpu.VMEM((size // 32, lanes), BF16),
    )


def body(*args):
    args = [a[0] for a in args]
    x, pre, _, fb, _, l1, r1, l2, r2 = args
    t, b = x.shape
    h = pre.shape[1]
    k = fb.shape[1]
    outs = [x, fb, fb, l1, r1, l2, r2]
    vm = pltpu.VMEM
    scratch = [
        vm((t, b), BF16), vm((t, b), BF16), vm((k, b, t), BF16), vm((k + 1, t, b), BF16),
        vm((t, h), BF16), vm((h, t), BF16), vm((t, h), F32), vm((t, h), F32),
        vm((k + 1, b, h), BF16), vm((k + 1, h, b), BF16), vm((t, h), BF16), vm((b, b), BF16),
        vm((b, b), BF16), vm((2 * b, t), BF16), vm((t, b), BF16), vm((5, t, b), BF16),
        vm((5, t, b), BF16), wide_buffers(t, b), sum_buffers(2 * b, t),
        wide_buffers(t, b),
        pltpu.SemaphoreType.DMA((20,)), pltpu.SemaphoreType.DMA((55,)),
        pltpu.SemaphoreType.DMA((11,)),
    ]
    results = pl.pallas_call(
        kernel,
        out_shape=[pltpu.VMEM(o.shape, o.dtype) for o in outs],
        in_specs=[pl.BlockSpec(memory_space=pl.ANY)] * 9,
        out_specs=[pl.BlockSpec(memory_space=pltpu.VMEM)] * 7,
        scratch_shapes=scratch,
        compiler_params=pltpu.CompilerParams(
            collective_id=0, has_side_effects=True, vmem_limit_bytes=50 * 1024 * 1024
        ),
    )(*args)
    results = pl.pallas_call(
        write_out,
        out_shape=[jax.ShapeDtypeStruct(o.shape, o.dtype) for o in outs],
        in_specs=[pl.BlockSpec(memory_space=pltpu.VMEM)] * 7,
        out_specs=[pl.BlockSpec(memory_space=pl.ANY)] * 7,
        scratch_shapes=[pltpu.SemaphoreType.DMA((7,))],
        compiler_params=pltpu.CompilerParams(vmem_limit_bytes=2 * 1024 * 1024),
    )(*[pltpu.with_memory_space_constraint(r, pltpu.VMEM) for r in results])
    return tuple(r[None] for r in results)


def solution(mesh):
    three = P("section", None, "tensor")
    rows = P("section", "tensor", None)
    blocks = P("section", "tensor", None, None, None)
    return jax.shard_map(
        body,
        mesh=mesh,
        in_specs=(three, three, three, blocks, blocks, rows, three, rows, three),
        out_specs=(three, blocks, blocks, rows, three, rows, three),
        check_vma=False,
    )
```

time: 122 us -> 84.5 us (0.69)
  Pallas kernels: 110 us -> 83.3 us
  local copies, waits for them, and re-layouts: 10.5 us -> 0 us
    pallas_call x1 -> x2, Pallas kernels: 110 us -> 83.3 us  [the longest x1 79.9 us: body(): pl.pallas_call(kernel, out_shape=[pltpu.VMEM(o.shape, o.dtype) for o in o...]
    unnamed x17 -> x0, local copies, waits for them, and re-layouts: 10.5 us -> none
where the time goes in v3:
time: 84.5 us; the launch traced here: 84.1 us
  Pallas kernels  83.3 us (99%)
    pallas_call x1, Pallas kernels, body(): pl.pallas_call(kernel, out_shape=[pltpu.VMEM(o.shape, o.dtype) for o in o...  79.9 us
    pallas_call x1, Pallas kernels, body(): pl.pallas_call(write_out, out_shape=[jax.ShapeDtypeStruct(o.shape, o.dtyp...  3.32 us

profile of v3, /device:TPU:1, one launch (start us, length us, event | category | flops | bytes accessed | tf_op | source)
XLA Modules:
  0.0 84.1 jit_solution(15672498656842177281)
XLA Ops:
  0.6 79.9 %shard_map.144 = (bf16[1024,256]{1,0:T(8,128)(2,1)S(1)}, bf16[4,6,256,256]{3,2,1,0:T(8,128)(2,1)S(1)}, bf16[4,6,256,256]{3,2,1,0:T(8,128)(2,1)S(1)}, bf16[256,25...) custom-call(bf16[1024,256]{1,0:T(8,128)(2,1)} %bitcast.19, ...), custom_call_target="tpu_custom_call" | custom-call | tf_op jit(solution)/shard_map/pallas_call | solution.py:477
  80.6 3.3 %shard_map.145 = (bf16[1024,256]{1,0:T(8,128)(2,1)}, bf16[4,6,256,256]{3,2,1,0:T(8,128)(2,1)}, bf16[4,6,256,256]{3,2,1,0:T(8,128)(2,1)}, bf16[256,256]{1,0:T(8,1...) custom-call(bf16[1024,256]{1,0:T(8,128)(2,1)S(1)} %get-tuple-element.21.refs_0_, ...), custom_call_target="tpu_custom_call" | custom-call | tf_op jit(solution)/shard_map/pallas_call | solution.py:487

commit v4 on v3

--- a/solution.py
+++ b/solution.py
@@ -329,14 +329,14 @@
     def both(h):
         return pl.ds(h * 2 * width, 2 * width)
 
-    def far_terms(h):
-        p_out[3, both(h), :] = nt(hid[both(h), :], w1[3]).astype(BF16)
-        p_out[4, both(h), :] = nt(hid[both(h), :], w1[5]).astype(BF16)
-
-    def far_sends(h):
-        for c in (2 * h, 2 * h + 1):
-            far2.append(send(p_out.at[3, rows(c)], p_in.at[3, rows(c)], peer[6], "p"))
-            far4.append(send(p_out.at[4, rows(c)], p_in.at[4, rows(c)], peer[24], "p"))
+    def far_terms(c):
+        left = hid[rows(c), :]
+        p_out[3, rows(c), :] = nt(left, w1[3]).astype(BF16)
+        p_out[4, rows(c), :] = nt(left, w1[5]).astype(BF16)
+
+    def far_sends(c):
+        far2.append(send(p_out.at[3, rows(c)], p_in.at[3, rows(c)], peer[6], "p"))
+        far4.append(send(p_out.at[4, rows(c)], p_in.at[4, rows(c)], peer[24], "p"))
 
     def near_terms(h):
         left = hid[both(h), :]
@@ -361,37 +361,39 @@
                 block = pl.ds(i * 256, 256)
                 fg[i, k] = nn(xt[k], hid[:, block]).astype(BF16)
 
-    for c in range(CHUNKS):
-        hidden(c)
+    hidden(0)
+    far_terms(0)
+    far_sends(0)
+    hidden(1)
+    far_terms(1)
+    far_sends(1)
+    hidden(2)
+    hidden(3)
     br_ar[0][...] = nt(hid[...], w1[6])
     back = summing_all(br_ar, br, "br")
     next(back)
-    next(pa)
-    far_terms(0)
+    far_terms(2)
     next(back)
-    next(pa)
-    far_sends(0)
+    far_sends(2)
+    next(pa)
+    far_terms(3)
+    far_sends(3)
     near_terms(0)
-    far_terms(1)
-    far_sends(1)
     near_terms(1)
     got("in", xt.at[pl.ds(0, 3)])
-    first_terms(0, 2)
     merge(0)
+    merge(1)
+    first_terms(0, 1)
     next(back)
+    first_terms(1, 2)
+    merge(2)
     first_terms(2, 3)
-    merge(1)
-    first_terms(3, 4)
-    next(pa)
-    merge(2)
-    first_terms(4, 5)
     merge(3)
-    first_terms(5, 6)
+    next(pa)
+    first_terms(3, 6)
     l2g[...] = nn(act_t[...], u[6]).astype(BF16)
     next(back)
     next(pa)
-    r1g[...] = nn(paf[pl.ds(0, 256), :], hid[...]).astype(BF16)
-    r2g[...] = nn(paf[pl.ds(256, 256), :], u[0]).astype(BF16)
     got("p", p_in.at[pl.ds(0, 3)])
     for c in range(CHUNKS):
         value = ga[rows(c), pl.ds(0, 256)]
@@ -401,6 +403,9 @@
     next(back)
     l1g[...] = nn(xt[0], br[...]).astype(BF16)
     ig[...] = (ga[:, pl.ds(0, 256)] + nt(br[...], l1[...])).astype(BF16)
+    next(pa)
+    r1g[...] = nn(paf[pl.ds(0, 256), :], hid[...]).astype(BF16)
+    r2g[...] = nn(paf[pl.ds(256, 256), :], u[0]).astype(BF16)
     sent("r2", r2)
     sent("hand", hand)
     sent("up", u.at[pl.ds(0, 5)])

time: 84.5 us -> 83.1 us (0.983)
  Pallas kernels: 83.3 us -> 82.2 us
    pallas_call x1, Pallas kernels: 79.9 us -> 78.9 us  [body(): pl.pallas_call(kernel, out_shape=[pltpu.VMEM(o.shape, o.dtype) for o in o...]
where the time goes in v4:
time: 83.1 us; the launch traced here: 83 us
  Pallas kernels  82.2 us (99%)
    pallas_call x1, Pallas kernels, body(): pl.pallas_call(kernel, out_shape=[pltpu.VMEM(o.shape, o.dtype) for o in o...  78.9 us
    pallas_call x1, Pallas kernels, body(): pl.pallas_call(write_out, out_shape=[jax.ShapeDtypeStruct(o.shape, o.dtyp...  3.32 us

profile of v4, /device:TPU:1, one launch (start us, length us, event | category | flops | bytes accessed | tf_op | source)
XLA Modules:
  0.0 83.0 jit_solution(701281969617463688)
XLA Ops:
  0.6 78.9 %shard_map.144 = (bf16[1024,256]{1,0:T(8,128)(2,1)S(1)}, bf16[4,6,256,256]{3,2,1,0:T(8,128)(2,1)S(1)}, bf16[4,6,256,256]{3,2,1,0:T(8,128)(2,1)S(1)}, bf16[256,25...) custom-call(bf16[1024,256]{1,0:T(8,128)(2,1)} %bitcast.19, ...), custom_call_target="tpu_custom_call" | custom-call | tf_op jit(solution)/shard_map/pallas_call | solution.py:482
  79.5 3.3 %shard_map.145 = (bf16[1024,256]{1,0:T(8,128)(2,1)}, bf16[4,6,256,256]{3,2,1,0:T(8,128)(2,1)}, bf16[4,6,256,256]{3,2,1,0:T(8,128)(2,1)}, bf16[256,256]{1,0:T(8,1...) custom-call(bf16[1024,256]{1,0:T(8,128)(2,1)S(1)} %get-tuple-element.21.refs_0_, ...), custom_call_target="tpu_custom_call" | custom-call | tf_op jit(solution)/shard_map/pallas_call | solution.py:492
